TPU v7x, 32 devices: a whole 2x2x4 slice. The times are simulated.
32 devices in a mesh: dp: 4 (over z), mp: 8 (over y, x, core).
Axes of the slice: x: 2, y: 2, z: 4, core: 2. Of those that a mesh axis runs over, the one named last changes fastest.
Arguments:
- tokens: bfloat16 [1024, 4096], P('dp', 'mp'), may hold values from -6 to 6
- weight_blocks: bfloat16 [2048, 4096], P('mp'), may hold values from -0.125 to 0.125
- block_rows: int32 [2048], P('mp'), may hold values from 0 to 63, as said below
- block_cols: int32 [2048], P('mp'), may hold values from 0 to 63, as said below
- importance: int32 [1024], P('dp'), may hold values from 1 to 64
- cotangent: bfloat16 [1024, 4096], P('dp', 'mp'), may hold values from -6 to 6
Outputs:
- projected: bfloat16 [1024, 4096], P('dp', 'mp')
- grad_input: bfloat16 [1024, 4096], P('dp', 'mp')
- grad_weight: bfloat16 [2048, 4096], P('mp')
Inputs may be any that keep to these rules, and one draw needn't show every extreme that they name: `block_rows`: with block_cols, each (row block, column block) pair appears at most once. `block_cols`: of the 256 blocks of one device, those in its own column blocks come first, then the others by owning device; at most 3 lie in the column blocks of any one other device, and in every draw some device's column blocks have exactly 3 blocks on every other device.
All inputs are finite; a program needn't handle non-finite values.
Results may differ from a plain program's by a relative error of at most 0.017.
Values may be sent and summed in bfloat16 or wider, within the bound.
A program may use at most 128 MiB of HBM per device.

v0:
```python
import math

import jax
import jax.numpy as jnp
from jax import lax
from jax.sharding import PartitionSpec as P

BLOCK = 64
CAP = 3


def group_view(array, groups):
    return array.reshape((groups, array.shape[0] // groups) + array.shape[1:])


def hot_sum(values, positions, segments):
    chosen = (positions[:, None] == jnp.arange(segments)[None, :]).astype(jnp.bfloat16)
    if values.dtype == jnp.bfloat16:
        return jnp.einsum("bnt,bc->cnt", values, chosen, preferred_element_type=jnp.float32)
    high = values.astype(jnp.bfloat16)
    low = (values - high.astype(jnp.float32)).astype(jnp.bfloat16)
    first = jnp.einsum("bnt,bc->cnt", high, chosen, preferred_element_type=jnp.float32)
    return first + jnp.einsum("bnt,bc->cnt", low, chosen, preferred_element_type=jnp.float32)


def per_device(tokens, weight_blocks, block_rows, block_cols, importance, cotangent):
    tok_count = tokens.shape[0]
    block_count = block_rows.shape[0]
    model_count = lax.axis_size("mp")
    data_count = lax.axis_size("dp")
    col_blocks = cotangent.shape[1] // BLOCK
    my_index = lax.axis_index("mp")
    slot_count = model_count * CAP
    groups = 4
    grad_scale = 1.0 / math.sqrt(tok_count * data_count)
    gathered = lax.all_gather(jnp.transpose(tokens), "mp", axis=0, tiled=True)
    row_blocks = gathered.shape[0] // BLOCK
    token_blocks = gathered.reshape(row_blocks, BLOCK, tok_count)
    token_taken = jnp.take(token_blocks, block_rows, axis=0)
    blocks = weight_blocks.reshape(block_count, BLOCK, BLOCK)
    local_col = block_cols - my_index * col_blocks
    at_home = (local_col >= 0) & (local_col < col_blocks)
    home_col = jnp.where(at_home, local_col, col_blocks)
    target = block_cols // col_blocks
    target_hot = (
        (target[:, None] == jnp.arange(model_count)[None, :]) & jnp.logical_not(at_home)[:, None]
    ).astype(jnp.int32)
    slot_rank = jnp.sum((jnp.cumsum(target_hot, axis=0) - target_hot) * target_hot, axis=1)
    slot_of = jnp.where(at_home, slot_count, target * CAP + slot_rank)
    owner_col = block_cols % col_blocks
    slot_match = slot_of[:, None] == jnp.arange(slot_count)[None, :]
    slot_used = jnp.any(slot_match, axis=0)
    slot_block = jnp.sum(jnp.where(slot_match, jnp.arange(block_count)[:, None], 0), axis=0)
    slot_pick = jnp.where(slot_used, slot_block, block_count)
    slot_col = jnp.where(
        slot_used, jnp.sum(jnp.where(slot_match, owner_col[:, None], 0), axis=0), col_blocks
    )
    weighted = importance.astype(jnp.float32) / 64.0
    grad_rows = (jnp.transpose(cotangent).astype(jnp.float32) * weighted[None, :]).astype(
        jnp.bfloat16
    )
    grad_rows = grad_rows.reshape(col_blocks, BLOCK, tok_count)
    empty_rows = jnp.zeros((1, BLOCK, tok_count), jnp.bfloat16)
    table_rows = jnp.concatenate([grad_rows, empty_rows])

    def forward_step(home_sum, pieces):
        token_part, weight_part, col_part = pieces
        partial_value = jnp.einsum(
            "bkt,bkn->bnt", token_part, weight_part, preferred_element_type=jnp.float32
        )
        home_sum = home_sum + hot_sum(partial_value, col_part, col_blocks + 1)
        return (home_sum, partial_value.astype(jnp.bfloat16))

    home_start = jnp.zeros((col_blocks + 1, BLOCK, tok_count), jnp.float32)
    home_sum, part_rounded = lax.scan(
        forward_step,
        home_start,
        (group_view(token_taken, groups), group_view(blocks, groups), group_view(home_col, groups)),
    )
    part_rounded = part_rounded.reshape(block_count, BLOCK, tok_count)
    outbox = jnp.take(jnp.concatenate([part_rounded, empty_rows]), slot_pick, axis=0)
    outbox = outbox.reshape(model_count, CAP, BLOCK, tok_count)
    in_parts, in_cols = (
        lax.all_to_all(outbox, "mp", split_axis=0, concat_axis=0, tiled=True),
        lax.all_to_all(
            slot_col.reshape(model_count, CAP), "mp", split_axis=0, concat_axis=0, tiled=True
        ),
    )
    in_cols = in_cols.reshape(slot_count)
    arrived = hot_sum(in_parts.reshape(slot_count, BLOCK, tok_count), in_cols, col_blocks + 1)
    replies = jnp.take(table_rows, in_cols, axis=0).reshape(model_count, CAP, BLOCK, tok_count)
    returned = lax.all_to_all(replies, "mp", split_axis=0, concat_axis=0, tiled=True)
    grad_table = jnp.concatenate([table_rows, returned.reshape(slot_count, BLOCK, tok_count)])
    grad_pick = jnp.where(at_home, home_col, col_blocks + 1 + slot_of)

    def backward_step(input_sum, pieces):
        token_part, weight_part, pick_part, row_part = pieces
        grad_blocks = jnp.take(grad_table, pick_part, axis=0)
        weight_grad = jnp.einsum(
            "bkt,bnt->bkn", token_part, grad_blocks, preferred_element_type=jnp.float32
        )
        input_part = jnp.einsum(
            "bnt,bkn->bkt", grad_blocks, weight_part, preferred_element_type=jnp.float32
        )
        input_sum = input_sum + hot_sum(input_part, row_part, row_blocks)
        return (input_sum, weight_grad.astype(jnp.bfloat16).reshape(-1, BLOCK * BLOCK))

    input_start = jnp.zeros((row_blocks, BLOCK, tok_count), jnp.float32)
    input_sum, weight_local = lax.scan(
        backward_step,
        input_start,
        (
            group_view(token_taken, groups),
            group_view(blocks, groups),
            group_view(grad_pick, groups),
            group_view(block_rows, groups),
        ),
    )
    weight_local = weight_local.reshape(block_count, BLOCK * BLOCK)
    weight_sum = lax.psum(weight_local, "dp").astype(jnp.float32)
    grad_weight = (weight_sum * grad_scale).astype(jnp.bfloat16)
    input_total = lax.psum_scatter(
        input_sum.astype(jnp.bfloat16), "mp", scatter_dimension=0, tiled=True
    ).astype(jnp.float32)
    grad_input = jnp.transpose(input_total.reshape(-1, tok_count)).astype(jnp.bfloat16)
    out_total = home_sum[:col_blocks] + arrived[:col_blocks]
    projected = jnp.transpose(out_total.reshape(col_blocks * BLOCK, tok_count)).astype(jnp.bfloat16)
    return (projected, grad_input, grad_weight)


def solution(mesh):
    return jax.shard_map(
        per_device,
        mesh=mesh,
        in_specs=(P("dp", "mp"), P("mp", None), P("mp"), P("mp"), P("dp"), P("dp", "mp")),
        out_specs=(P("dp", "mp"), P("dp", "mp"), P("mp", None)),
        check_vma=False,
    )
```

profile of v0, /device:TPU:0, one launch (start us, length us, event | category | flops | bytes accessed | tf_op | source)
XLA Modules:
  0.0 290.4 jit_solution(1843964331724299790)
XLA Ops:
  7.2 1.8 copy.60
  11.4 0.7 add_select_fusion
  13.0 5.2 %all-to-all-start = ((s32[8,1,3]{2,1,0:T(1,128)}), s32[8,1,3]{2,1,0:T(1,128)S(1)}, u32[]{:S(2)}, u32[]{:S(2)}) async-start(s32[8,1,3]{2,1,0:T(1,128)} %bitcast.7), calls=%async_computation | async-start | bytes 8192 | tf_op jit(solution)/shard_map/all_to_all | solution.py:85
  18.9 1.1 fusion.47
  20.1 2.7 all-to-all-done
  23.7 1.0 broadcast_select_fusion.4
  24.7 3.5 %all-to-all-start.2 = ((bf16[8,3,64,256]{3,2,1,0:T(8,128)(2,1)}), bf16[8,3,64,256]{3,2,1,0:T(8,128)(2,1)S(1)}, u32[]{:S(2)}, u32[]{:S(2)}) async-start(bf16[8,3,64,256]{3,2,1,0:T(8,128)(2,1)} %broadcast_select_fusion.4), calls=%async_computation.2 | async-start | bytes 1572864 | tf_op jit(solution)/shard_map/all_to_all | solution.py:92
  28.3 6.9 %reshape_reshape.4 = bf16[4,64,64,64]{3,2,1,0:T(8,128)(2,1)} reshape(bf16[256,4096]{1,0:T(8,128)(2,1)} %param.11) | data formatting | bytes 4194304 | tf_op jit(solution)/shard_map/reshape;reshape | solution.py:13
  35.6 10.7 %all-to-all-done.2 = bf16[8,3,64,256]{3,2,1,0:T(8,128)(2,1)S(1)} async-done(((bf16[8,3,64,256]{3,2,1,0:T(8,128)(2,1)}), bf16[8,3,64,256]{3,2,1,0:T(8,128)(2,1)S(1)}, u32[]{:S(2)}, u32[]{:S(2)}) %all-to-all-start.2) | async-done | bytes 786464 | tf_op jit(solution)/shard_map/all_to_all | solution.py:92
  46.5 10.3 %gather_fusion.1 = bf16[256,64,256]{2,1,0:T(8,128)(2,1)} fusion(bf16[64,64,256]{2,1,0:T(8,128)(2,1)} %bitcast.111, s32[1024]{0:T(1024)S(1)} %pad_clamp_fusion.3), kind=kCustom, calls=%fused_computation.1 | custom fusion | bytes 16778240 | tf_op jit(solution)/shard_map/jit(_take)/gather | solution.py:39
  56.8 7.5 %broadcast_select_fusion.3 = bf16[4,64,64,256]{3,2,1,0:T(8,128)(2,1)} fusion(bf16[4,64,64,256]{3,2,1,0:T(8,128)(2,1)} %bitcast.110, pred[4,64]{1,0:T(4,128)(4,1)S(1)} %broadcast_in_dim.113), kind=kLoop, calls=%fused_computation.54 | loop fusion | flops 4194304 | bytes 16777472 | tf_op jit(solution)/shard_map/jit(_take)/select_n | solution.py:39
  64.3 87.2 %while.27 = (s32[]{:T(128)}, f32[64,64,256]{2,0,1:T(8,128)}, bf16[4,64,4096]{2,1,0:T(8,128)(2,1)}, s32[4,64]{1,0:T(4,128)S(1)}, bf16[4,64,64,64]{3,2,1,0:T(8,128...) while((s32[]{:T(128)}, f32[64,64,256]{2,0,1:T(8,128)}, ...), condition=%wide.region_9.10_spmd.clone, body=%wide.region_8.9_spmd.clone.sunk | while | flops 546580032 | bytes 39328332 | solution.py:109
  65.0 3.4 %subtract_convert_fusion.5 = (bf16[64,64,256]{2,1,0:T(8,128)(2,1)}, bf16[64,64,256]{2,1,0:T(8,128)(2,1)S(1)}) fusion(bf16[64,64,256]{2,1,0:T(8,128)(2,1)S(1)} %gather_fusion, pred[64]{0:T(512)(128)(4,1)S(1)} %compare_and_fusion.7, bf16[4,64,64,64]{3,2,1,0:T(8,128)(2,1)} %get-tuple-element.352, s32[]{:T(128)S(6)} %copy.112), kind=kOutput, calls=%fused_computation.25.clone.1 | convolution fusion | flops 139460608 | bytes 7340100 | tf_op jit(solution)/shard_map/while/body/eval_jaxpr/bnt,bkn->bkt/dot_general | solution.py:102
  68.4 3.7 %fusion.89 = f32[64,64,256]{2,0,1:T(8,128)} fusion(bf16[64,64,256]{2,1,0:T(8,128)(2,1)S(1)} %get-tuple-element.302, s32[64]{0:T(128)S(1)} %fusion.88), kind=kOutput, calls=%fused_computation.29.clone.1 | convolution fusion | flops 134221824 | bytes 6291712 | tf_op jit(solution)/shard_map/while/body/eval_jaxpr/bnt,bc->cnt/dot_general | solution.py:22
  72.1 6.8 %select_add_fusion.2 = f32[64,64,256]{2,0,1:T(8,128)} fusion(f32[64,64,256]{2,0,1:T(8,128)} %get-tuple-element.339, f32[64,64,256]{2,0,1:T(8,128)} %fusion.89, bf16[64,64,256]{2,1,0:T(8,128)(2,1)} %get-tuple-element.303, pred[]{:T(512)S(6)} %compare.12, s32[64]{0:T(128)S(1)} %fusion.88), kind=kOutput, calls=%fused_computation.24.clone.1 | convolution fusion | flops 137367552 | bytes 14680321 | tf_op jit(solution)/shard_map/while/body/eval_jaxpr/bnt,bc->cnt/dot_general | solution.py:23
  78.9 3.4 %fusion.90 = bf16[64,64,64]{2,1,0:T(8,128)(2,1)} fusion(bf16[4,64,64,256]{3,2,1,0:T(8,128)(2,1)} %get-tuple-element.355, s32[]{:T(128)S(6)} %copy.112, bf16[64,64,256]{2,1,0:T(8,128)(2,1)S(1)} %gather_fusion, pred[64]{0:T(512)(128)(4,1)S(1)} %compare_and_fusion.7), kind=kOutput, calls=%fused_computation.33.clone.1 | convolution fusion | flops 135528448 | bytes 4718660 | tf_op jit(solution)/shard_map/while/body/eval_jaxpr/bkt,bnt->bkn/dot_general | solution.py:99
  82.3 2.1 broadcast_in_dim.169
  84.4 0.8 constant_dynamic-update-slice_fusion.2
  85.9 3.4 %subtract_convert_fusion.5 = (bf16[64,64,256]{2,1,0:T(8,128)(2,1)}, bf16[64,64,256]{2,1,0:T(8,128)(2,1)S(1)}) fusion(bf16[64,64,256]{2,1,0:T(8,128)(2,1)S(1)} %gather_fusion, pred[64]{0:T(512)(128)(4,1)S(1)} %compare_and_fusion.7, bf16[4,64,64,64]{3,2,1,0:T(8,128)(2,1)} %get-tuple-element.352, s32[]{:T(128)S(6)} %copy.112), kind=kOutput, calls=%fused_computation.25.clone.1 | convolution fusion | flops 139460608 | bytes 7340100 | tf_op jit(solution)/shard_map/while/body/eval_jaxpr/bnt,bkn->bkt/dot_general | solution.py:102
  89.3 3.7 %fusion.89 = f32[64,64,256]{2,0,1:T(8,128)} fusion(bf16[64,64,256]{2,1,0:T(8,128)(2,1)S(1)} %get-tuple-element.302, s32[64]{0:T(128)S(1)} %fusion.88), kind=kOutput, calls=%fused_computation.29.clone.1 | convolution fusion | flops 134221824 | bytes 6291712 | tf_op jit(solution)/shard_map/while/body/eval_jaxpr/bnt,bc->cnt/dot_general | solution.py:22
  92.9 8.0 %select_add_fusion.2 = f32[64,64,256]{2,0,1:T(8,128)} fusion(f32[64,64,256]{2,0,1:T(8,128)} %get-tuple-element.339, f32[64,64,256]{2,0,1:T(8,128)} %fusion.89, bf16[64,64,256]{2,1,0:T(8,128)(2,1)} %get-tuple-element.303, pred[]{:T(512)S(6)} %compare.12, s32[64]{0:T(128)S(1)} %fusion.88), kind=kOutput, calls=%fused_computation.24.clone.1 | convolution fusion | flops 137367552 | bytes 14680321 | tf_op jit(solution)/shard_map/while/body/eval_jaxpr/bnt,bc->cnt/dot_general | solution.py:23
  101.0 3.4 %fusion.90 = bf16[64,64,64]{2,1,0:T(8,128)(2,1)} fusion(bf16[4,64,64,256]{3,2,1,0:T(8,128)(2,1)} %get-tuple-element.355, s32[]{:T(128)S(6)} %copy.112, bf16[64,64,256]{2,1,0:T(8,128)(2,1)S(1)} %gather_fusion, pred[64]{0:T(512)(128)(4,1)S(1)} %compare_and_fusion.7), kind=kOutput, calls=%fused_computation.33.clone.1 | convolution fusion | flops 135528448 | bytes 4718660 | tf_op jit(solution)/shard_map/while/body/eval_jaxpr/bkt,bnt->bkn/dot_general | solution.py:99
  104.4 2.1 broadcast_in_dim.169
  106.5 0.8 constant_dynamic-update-slice_fusion.2
  108.0 3.4 %subtract_convert_fusion.5 = (bf16[64,64,256]{2,1,0:T(8,128)(2,1)}, bf16[64,64,256]{2,1,0:T(8,128)(2,1)S(1)}) fusion(bf16[64,64,256]{2,1,0:T(8,128)(2,1)S(1)} %gather_fusion, pred[64]{0:T(512)(128)(4,1)S(1)} %compare_and_fusion.7, bf16[4,64,64,64]{3,2,1,0:T(8,128)(2,1)} %get-tuple-element.352, s32[]{:T(128)S(6)} %copy.112), kind=kOutput, calls=%fused_computation.25.clone.1 | convolution fusion | flops 139460608 | bytes 7340100 | tf_op jit(solution)/shard_map/while/body/eval_jaxpr/bnt,bkn->bkt/dot_general | solution.py:102
  111.4 3.7 %fusion.89 = f32[64,64,256]{2,0,1:T(8,128)} fusion(bf16[64,64,256]{2,1,0:T(8,128)(2,1)S(1)} %get-tuple-element.302, s32[64]{0:T(128)S(1)} %fusion.88), kind=kOutput, calls=%fused_computation.29.clone.1 | convolution fusion | flops 134221824 | bytes 6291712 | tf_op jit(solution)/shard_map/while/body/eval_jaxpr/bnt,bc->cnt/dot_general | solution.py:22
  115.0 8.0 %select_add_fusion.2 = f32[64,64,256]{2,0,1:T(8,128)} fusion(f32[64,64,256]{2,0,1:T(8,128)} %get-tuple-element.339, f32[64,64,256]{2,0,1:T(8,128)} %fusion.89, bf16[64,64,256]{2,1,0:T(8,128)(2,1)} %get-tuple-element.303, pred[]{:T(512)S(6)} %compare.12, s32[64]{0:T(128)S(1)} %fusion.88), kind=kOutput, calls=%fused_computation.24.clone.1 | convolution fusion | flops 137367552 | bytes 14680321 | tf_op jit(solution)/shard_map/while/body/eval_jaxpr/bnt,bc->cnt/dot_general | solution.py:23
  123.1 3.4 %fusion.90 = bf16[64,64,64]{2,1,0:T(8,128)(2,1)} fusion(bf16[4,64,64,256]{3,2,1,0:T(8,128)(2,1)} %get-tuple-element.355, s32[]{:T(128)S(6)} %copy.112, bf16[64,64,256]{2,1,0:T(8,128)(2,1)S(1)} %gather_fusion, pred[64]{0:T(512)(128)(4,1)S(1)} %compare_and_fusion.7), kind=kOutput, calls=%fused_computation.33.clone.1 | convolution fusion | flops 135528448 | bytes 4718660 | tf_op jit(solution)/shard_map/while/body/eval_jaxpr/bkt,bnt->bkn/dot_general | solution.py:99
  126.5 2.1 broadcast_in_dim.169
  128.6 0.8 constant_dynamic-update-slice_fusion.2
  130.1 3.4 %subtract_convert_fusion.5 = (bf16[64,64,256]{2,1,0:T(8,128)(2,1)}, bf16[64,64,256]{2,1,0:T(8,128)(2,1)S(1)}) fusion(bf16[64,64,256]{2,1,0:T(8,128)(2,1)S(1)} %gather_fusion, pred[64]{0:T(512)(128)(4,1)S(1)} %compare_and_fusion.7, bf16[4,64,64,64]{3,2,1,0:T(8,128)(2,1)} %get-tuple-element.352, s32[]{:T(128)S(6)} %copy.112), kind=kOutput, calls=%fused_computation.25.clone.1 | convolution fusion | flops 139460608 | bytes 7340100 | tf_op jit(solution)/shard_map/while/body/eval_jaxpr/bnt,bkn->bkt/dot_general | solution.py:102
  133.5 3.7 %fusion.89 = f32[64,64,256]{2,0,1:T(8,128)} fusion(bf16[64,64,256]{2,1,0:T(8,128)(2,1)S(1)} %get-tuple-element.302, s32[64]{0:T(128)S(1)} %fusion.88), kind=kOutput, calls=%fused_computation.29.clone.1 | convolution fusion | flops 134221824 | bytes 6291712 | tf_op jit(solution)/shard_map/while/body/eval_jaxpr/bnt,bc->cnt/dot_general | solution.py:22
  137.1 8.0 %select_add_fusion.2 = f32[64,64,256]{2,0,1:T(8,128)} fusion(f32[64,64,256]{2,0,1:T(8,128)} %get-tuple-element.339, f32[64,64,256]{2,0,1:T(8,128)} %fusion.89, bf16[64,64,256]{2,1,0:T(8,128)(2,1)} %get-tuple-element.303, pred[]{:T(512)S(6)} %compare.12, s32[64]{0:T(128)S(1)} %fusion.88), kind=kOutput, calls=%fused_computation.24.clone.1 | convolution fusion | flops 137367552 | bytes 14680321 | tf_op jit(solution)/shard_map/while/body/eval_jaxpr/bnt,bc->cnt/dot_general | solution.py:23
  145.2 3.4 %fusion.90 = bf16[64,64,64]{2,1,0:T(8,128)(2,1)} fusion(bf16[4,64,64,256]{3,2,1,0:T(8,128)(2,1)} %get-tuple-element.355, s32[]{:T(128)S(6)} %copy.112, bf16[64,64,256]{2,1,0:T(8,128)(2,1)S(1)} %gather_fusion, pred[64]{0:T(512)(128)(4,1)S(1)} %compare_and_fusion.7), kind=kOutput, calls=%fused_computation.33.clone.1 | convolution fusion | flops 135528448 | bytes 4718660 | tf_op jit(solution)/shard_map/while/body/eval_jaxpr/bkt,bnt->bkn/dot_general | solution.py:99
  148.6 2.1 broadcast_in_dim.169
  150.7 0.8 constant_dynamic-update-slice_fusion.2
  152.0 5.7 %copy.89 = bf16[64,64,256]{2,1,0:T(8,128)(2,1)} copy(f32[64,64,256]{2,0,1:T(8,128)} %get-tuple-element.81) | data formatting | bytes 6291456 | tf_op jit(solution)/shard_map/while | solution.py:109
  157.7 37.6 %while.26 = (s32[]{:T(128)}, f32[9,64,256]{2,0,1:T(8,128)}, bf16[4,64,64,256]{3,2,1,0:T(8,128)(2,1)}, s32[4,64]{1,0:T(4,128)S(1)}, bf16[4,64,64,64]{3,2,1,0:T(8,...) while((s32[]{:T(128)}, f32[9,64,256]{2,0,1:T(8,128)}, ...), condition=%wide.region_1.2_spmd.clone, body=%wide.region_0.1_spmd.clone.sunk | while | flops 176604288 | bytes 26479208 | solution.py:75
  157.7 4.1 %bitcast_dynamic-update-slice_fusion.2 = (bf16[4,64,64,256]{3,2,1,0:T(8,128)(2,1)}, bf16[64,64,256]{2,1,0:T(8,128)(2,1)S(1)}, f32[64,64,256]{2,1,0:T(8,128)S(1)}) fusion(bf16[4,64,64,256]{3,2,1,0:T(8,128)(2,1)} %get-tuple-element.314, s32[]{:T(128)S(6)} %copy.103, bf16[4,64,64,256]{3,2,1,0:T(8,128)(2,1)} %get-tuple-element.325, ...), kind=kOutput, calls=%fused_computation.5.clone.1 | convolution fusion | flops 135266304 | bytes 11535872 | tf_op jit(solution)/shard_map/while/body/eval_jaxpr/bkt,bkn->bnt/dot_general | solution.py:68
  161.8 0.8 subtract_convert_fusion.4
  162.7 1.2 fusion.80
  163.9 2.3 fusion.81
  166.2 4.1 %bitcast_dynamic-update-slice_fusion.2 = (bf16[4,64,64,256]{3,2,1,0:T(8,128)(2,1)}, bf16[64,64,256]{2,1,0:T(8,128)(2,1)S(1)}, f32[64,64,256]{2,1,0:T(8,128)S(1)}) fusion(bf16[4,64,64,256]{3,2,1,0:T(8,128)(2,1)} %get-tuple-element.314, s32[]{:T(128)S(6)} %copy.103, bf16[4,64,64,256]{3,2,1,0:T(8,128)(2,1)} %get-tuple-element.325, ...), kind=kOutput, calls=%fused_computation.5.clone.1 | convolution fusion | flops 135266304 | bytes 11535872 | tf_op jit(solution)/shard_map/while/body/eval_jaxpr/bkt,bkn->bnt/dot_general | solution.py:68
  170.3 0.8 subtract_convert_fusion.4
  171.2 1.2 fusion.80
  172.4 3.5 %fusion.81 = f32[9,64,256]{2,0,1:T(8,128)} fusion(f32[9,64,256]{2,0,1:T(8,128)S(1)} %fusion.80, bf16[64,64,256]{2,1,0:T(8,128)(2,1)S(1)} %get-tuple-element.292, f32[9,64,256]{2,0,1:T(8,128)} %get-tuple-element.313, pred[]{:T(512)S(6)} %compare.11, s32[64]{0:T(128)S(1)} %fusion.79), kind=kOutput, calls=%fused_computation.14.clone.1 | convolution fusion | flops 19317312 | bytes 3866881 | tf_op jit(solution)/shard_map/while/body/eval_jaxpr/bnt,bc->cnt/dot_general | solution.py:22
  175.9 4.0 %bitcast_dynamic-update-slice_fusion.2 = (bf16[4,64,64,256]{3,2,1,0:T(8,128)(2,1)}, bf16[64,64,256]{2,1,0:T(8,128)(2,1)S(1)}, f32[64,64,256]{2,1,0:T(8,128)S(1)}) fusion(bf16[4,64,64,256]{3,2,1,0:T(8,128)(2,1)} %get-tuple-element.314, s32[]{:T(128)S(6)} %copy.103, bf16[4,64,64,256]{3,2,1,0:T(8,128)(2,1)} %get-tuple-element.325, ...), kind=kOutput, calls=%fused_computation.5.clone.1 | convolution fusion | flops 135266304 | bytes 11535872 | tf_op jit(solution)/shard_map/while/body/eval_jaxpr/bkt,bkn->bnt/dot_general | solution.py:68
  179.9 0.8 subtract_convert_fusion.4
  180.8 1.2 fusion.80
  182.0 3.5 %fusion.81 = f32[9,64,256]{2,0,1:T(8,128)} fusion(f32[9,64,256]{2,0,1:T(8,128)S(1)} %fusion.80, bf16[64,64,256]{2,1,0:T(8,128)(2,1)S(1)} %get-tuple-element.292, f32[9,64,256]{2,0,1:T(8,128)} %get-tuple-element.313, pred[]{:T(512)S(6)} %compare.11, s32[64]{0:T(128)S(1)} %fusion.79), kind=kOutput, calls=%fused_computation.14.clone.1 | convolution fusion | flops 19317312 | bytes 3866881 | tf_op jit(solution)/shard_map/while/body/eval_jaxpr/bnt,bc->cnt/dot_general | solution.py:22
  185.6 4.1 %bitcast_dynamic-update-slice_fusion.2 = (bf16[4,64,64,256]{3,2,1,0:T(8,128)(2,1)}, bf16[64,64,256]{2,1,0:T(8,128)(2,1)S(1)}, f32[64,64,256]{2,1,0:T(8,128)S(1)}) fusion(bf16[4,64,64,256]{3,2,1,0:T(8,128)(2,1)} %get-tuple-element.314, s32[]{:T(128)S(6)} %copy.103, bf16[4,64,64,256]{3,2,1,0:T(8,128)(2,1)} %get-tuple-element.325, ...), kind=kOutput, calls=%fused_computation.5.clone.1 | convolution fusion | flops 135266304 | bytes 11535872 | tf_op jit(solution)/shard_map/while/body/eval_jaxpr/bkt,bkn->bnt/dot_general | solution.py:68
  189.7 0.8 subtract_convert_fusion.4
  190.5 1.2 fusion.80
  191.8 3.5 %fusion.81 = f32[9,64,256]{2,0,1:T(8,128)} fusion(f32[9,64,256]{2,0,1:T(8,128)S(1)} %fusion.80, bf16[64,64,256]{2,1,0:T(8,128)(2,1)S(1)} %get-tuple-element.292, f32[9,64,256]{2,0,1:T(8,128)} %get-tuple-element.313, pred[]{:T(512)S(6)} %compare.11, s32[64]{0:T(128)S(1)} %fusion.79), kind=kOutput, calls=%fused_computation.14.clone.1 | convolution fusion | flops 19317312 | bytes 3866881 | tf_op jit(solution)/shard_map/while/body/eval_jaxpr/bnt,bc->cnt/dot_general | solution.py:22
  195.3 8.3 %concatenate.10 = bf16[257,64,256]{2,1,0:T(8,128)(2,1)} pad(bf16[256,64,256]{2,1,0:T(8,128)(2,1)} %bitcast.112, bf16[]{:T(256)} %constant.122.clone.1), padding=0_1x0_0x0_0 | pad | bytes 16809986 | tf_op jit(solution)/shard_map/concatenate | solution.py:81
  203.6 4.1 %gather_fusion.2 = bf16[24,64,256]{2,1,0:T(8,128)(2,1)S(1)} fusion(bf16[257,64,256]{2,1,0:T(8,128)(2,1)} %concatenate.10, s32[1024]{0:T(1024)S(1)} %pad_clamp_fusion.2), kind=kCustom, calls=%fused_computation.2 | custom fusion | bytes 1572960 | tf_op jit(solution)/shard_map/jit(_take)/gather | solution.py:81
  207.7 1.0 broadcast_select_fusion.5
  208.7 3.5 %all-to-all-start.1 = ((bf16[8,3,64,256]{3,2,1,0:T(8,128)(2,1)}), bf16[8,3,64,256]{3,2,1,0:T(8,128)(2,1)S(1)}, u32[]{:S(2)}, u32[]{:S(2)}) async-start(bf16[8,3,64,256]{3,2,1,0:T(8,128)(2,1)} %broadcast_select_fusion.5), calls=%async_computation.1 | async-start | bytes 1572864 | tf_op jit(solution)/shard_map/all_to_all | solution.py:84
  213.5 11.2 %all-to-all-done.1 = bf16[8,3,64,256]{3,2,1,0:T(8,128)(2,1)S(1)} async-done(((bf16[8,3,64,256]{3,2,1,0:T(8,128)(2,1)}), bf16[8,3,64,256]{3,2,1,0:T(8,128)(2,1)S(1)}, u32[]{:S(2)}, u32[]{:S(2)}) %all-to-all-start.1) | async-done | bytes 786464 | tf_op jit(solution)/shard_map/all_to_all | solution.py:84
  225.5 0.8 copy.71
  226.3 12.3 %all-reduce.4.cloned.1.call-done = bf16[256,4096]{1,0:T(8,128)(2,1)} async-done(((bf16[256,4096]{1,0:T(8,128)(2,1)}), bf16[256,4096]{1,0:T(8,128)(2,1)}) %all-reduce.4.cloned.1.call-update) | async-done | bytes 2097168 | tf_op jit(solution)/shard_map/psum | solution.py:120
  238.6 3.3 %multiply_convert_fusion = bf16[256,4096]{1,0:T(8,128)(2,1)} fusion(bf16[256,4096]{1,0:T(8,128)(2,1)} %all-reduce.4.cloned.1.call-done), kind=kLoop, calls=%fused_computation.56 | loop fusion | flops 3145728 | bytes 4194304 | tf_op jit(solution)/shard_map/convert_element_type | solution.py:121
  241.9 40.1 %reduce-scatter.2.cloned.1.call-done = bf16[8,64,256]{2,1,0:T(8,128)(2,1)} async-done(((bf16[64,64,256]{2,1,0:T(8,128)(2,1)}), bf16[8,64,256]{2,1,0:T(8,128)(2,1)}) %reduce-scatter.2.cloned.1.call-update) | async-done | bytes 262160 | tf_op jit(solution)/shard_map/reduce_scatter | solution.py:122
  282.1 1.8 copy.72
  (81 shorter events, 10.9 us)
Async XLA Ops:
  7.2 39.3 %all-gather.2.cloned.1.call-start = ((), (), s32[]{:S(2)}) async-start(), calls=%async_computation.4 | async-start | bytes 2359296 | tf_op jit(solution)/shard_map/all_gather | solution.py:36
  13.0 9.8 %all-to-all-start = ((s32[8,1,3]{2,1,0:T(1,128)}), s32[8,1,3]{2,1,0:T(1,128)S(1)}, u32[]{:S(2)}, u32[]{:S(2)}) async-start(s32[8,1,3]{2,1,0:T(1,128)} %bitcast.7), calls=%async_computation | async-start | bytes 8192 | tf_op jit(solution)/shard_map/all_to_all | solution.py:85
  24.7 21.6 %all-to-all-start.2 = ((bf16[8,3,64,256]{3,2,1,0:T(8,128)(2,1)}), bf16[8,3,64,256]{3,2,1,0:T(8,128)(2,1)S(1)}, u32[]{:S(2)}, u32[]{:S(2)}) async-start(bf16[8,3,64,256]{3,2,1,0:T(8,128)(2,1)} %broadcast_select_fusion.4), calls=%async_computation.2 | async-start | bytes 1572864 | tf_op jit(solution)/shard_map/all_to_all | solution.py:92
  28.3 210.3 %all-reduce.4.cloned.1.call-start = ((), (), s32[]{:S(2)}) async-start(), calls=%async_computation.6 | async-start | bytes 4194304 | tf_op jit(solution)/shard_map/psum | solution.py:120
  28.3 6.9 %copy-start.1 = (s32[256]{0:T(256)S(1)}, s32[256]{0:T(256)}, u32[]{:S(2)}) copy-start(s32[256]{0:T(256)} %param.12) | copy-start | bytes 3076
  151.5 130.5 %reduce-scatter.2.cloned.1.call-start = ((), (), s32[]{:S(2)}) async-start(), calls=%async_computation.5 | async-start | bytes 2359296 | tf_op jit(solution)/shard_map/reduce_scatter | solution.py:122
  203.6 21.2 %copy-start = (f32[9,64,256]{2,0,1:T(8,128)S(1)}, f32[9,64,256]{2,0,1:T(8,128)}, u32[]{:S(2)}) copy-start(f32[9,64,256]{2,0,1:T(8,128)} %get-tuple-element.79) | copy-start | bytes 1769476
  208.7 16.1 %all-to-all-start.1 = ((bf16[8,3,64,256]{3,2,1,0:T(8,128)(2,1)}), bf16[8,3,64,256]{3,2,1,0:T(8,128)(2,1)S(1)}, u32[]{:S(2)}, u32[]{:S(2)}) async-start(bf16[8,3,64,256]{3,2,1,0:T(8,128)(2,1)} %broadcast_select_fusion.5), calls=%async_computation.1 | async-start | bytes 1572864 | tf_op jit(solution)/shard_map/all_to_all | solution.py:84
Sparse Core Ops, SparseCore 0:
  10.4 36.0 all-gather.1
  151.6 86.9 all-reduce.3
  241.9 40.1 reduce-scatter.1
where the time goes:
time: 292 us; the launch traced here: 290 us
  matrix products  107 us (37%)
  waiting for transfers between devices  77.1 us (26%)
  local copies, waits for them, and re-layouts  57.1 us (20%)
  other arithmetic  22 us (8%)
  between operations  13.9 us (5%)
  starting transfers between devices  12.6 us (4%)
    reduce_scatter x1, waiting for transfers between devices, per_device(): lax.psum_scatter(input_sum.astype(jnp.bfloat16), 'mp', scatter_dimension=...  40.1 us
    dot_general x8, matrix products, hot_sum(): jnp.einsum('bnt,bc->cnt', low, chosen, preferred_element_type=jnp.float32)  35.8 us
    dot_general x8, matrix products, hot_sum(): jnp.einsum('bnt,bc->cnt', high, chosen, preferred_element_type=jnp.float32)  27.5 us
    dot_general x4, matrix products, forward_step(): jnp.einsum('bkt,bkn->bnt', token_part, weight_part, preferred_element_typ...  16.3 us
    dot_general x4, matrix products, backward_step(): jnp.einsum('bkt,bnt->bkn', token_part, grad_blocks, preferred_element_typ...  13.7 us
    dot_general x4, matrix products, backward_step(): jnp.einsum('bnt,bkn->bkt', grad_blocks, weight_part, preferred_element_ty...  13.4 us
    psum x1, waiting for transfers between devices, per_device(): weight_sum = lax.psum(weight_local, 'dp').astype(jnp.float32)  12.3 us
    all_to_all x1, waiting for transfers between devices, per_device(): lax.all_to_all(outbox, 'mp', split_axis=0, concat_axis=0, tiled=True)  11.2 us
  transfers between devices with their start and end apart: 6, of which 5 were waited for; matrix products, arithmetic and copies ran while one was open for 27% of the time, Pallas kernels for 0%

commit v1 on v0

v1 whole, which is shorter than its diff:
```python
import functools
import math

import jax
import jax.numpy as jnp
from jax import lax
from jax.experimental import pallas as pl
from jax.experimental.pallas import tpu as pltpu
from jax.sharding import PartitionSpec as P

BLOCK = 64
CAP = 3
GROUP = 8


def mm(a, b, dims=((1,), (0,))):
    return lax.dot_general(a, b, (dims, ((), ())), preferred_element_type=jnp.float32)


def swap_halves(x, y):
    width = x.shape[1]
    low = (lax.broadcasted_iota(jnp.int32, x.shape, 1) % 128) < 64
    first = jnp.where(low, x, pltpu.roll(y, 64, 1))
    second = jnp.where(low, pltpu.roll(x, width - 64, 1), y)
    return first, second


def dense_kernel(tok_ref, up_ref, w_ref, win_ref, crow_ref, crow_in_ref, ccol_ref, ccol_in_ref,
                 proj_ref, gi_ref, gw_ref, gw_in_ref,
                 wc_ref, wd_ref, gc_ref, gd_ref, acc_ref):
    d_count, tok_count, feat = tok_ref.shape
    cols = up_ref.shape[1]
    col_blocks = cols // BLOCK
    span = GROUP * BLOCK
    per = span // feat
    chunks = d_count // per
    cells = GROUP * col_blocks
    flat = BLOCK * BLOCK
    pairs = col_blocks // 2
    quads = BLOCK // 2
    src = lax.broadcasted_iota(jnp.int32, (span, span), 0)
    dst = lax.broadcasted_iota(jnp.int32, (span, span), 1)
    perm = ((src % BLOCK) * GROUP + src // BLOCK == dst).astype(jnp.float32).astype(jnp.bfloat16)
    acc_ref[...] = jnp.zeros_like(acc_ref)

    def chunk(j, _):
        base = j * cells
        ids = lax.broadcasted_iota(jnp.int32, (cells, 1), 0) + base
        hot = (ids == crow_ref[...]).astype(jnp.float32).astype(jnp.bfloat16)
        hot_in = (ids == crow_in_ref[...]).astype(jnp.float32).astype(jnp.bfloat16)
        wc_ref[...] = mm(hot, w_ref[...]) + mm(hot_in, win_ref[...])
        for p in range(pairs):
            a = wc_ref[2 * GROUP * p : 2 * GROUP * p + GROUP, :]
            b = wc_ref[2 * GROUP * p + GROUP : 2 * GROUP * (p + 1), :]
            even, odd = swap_halves(a, b)
            for q in range(quads):
                both = jnp.concatenate(
                    [even[:, 128 * q : 128 * (q + 1)], odd[:, 128 * q : 128 * (q + 1)]], axis=0
                )
                wd_ref[2 * GROUP * q : 2 * GROUP * (q + 1), 128 * p : 128 * (p + 1)] = both.astype(
                    jnp.bfloat16
                )
        parts = [tok_ref[j * per + g] for g in range(per)]
        tok = parts[0] if per == 1 else jnp.concatenate(parts, axis=1)
        tok_p = mm(tok, perm).astype(jnp.bfloat16)
        tok_t = mm(perm, tok, ((0,), (1,))).astype(jnp.bfloat16)
        acc_ref[...] += mm(tok_p, wd_ref[...])
        gi_p = mm(up_ref[...], wd_ref[...], ((1,), (1,))).astype(jnp.bfloat16)
        gi = mm(gi_p, perm, ((1,), (1,))).astype(jnp.bfloat16)
        for g in range(per):
            gi_ref[j * per + g] = gi[:, g * feat : (g + 1) * feat]
        gd_ref[...] = mm(tok_t, up_ref[...])
        for p in range(pairs):
            for q in range(quads):
                x = gd_ref[2 * GROUP * q : 2 * GROUP * q + GROUP, 128 * p : 128 * (p + 1)]
                y = gd_ref[2 * GROUP * q + GROUP : 2 * GROUP * (q + 1), 128 * p : 128 * (p + 1)]
                a, b = swap_halves(x, y)
                gc_ref[
                    pl.ds(pl.multiple_of(base + 2 * GROUP * p, 2 * GROUP), 2 * GROUP),
                    128 * q : 128 * (q + 1),
                ] = jnp.concatenate([a, b], axis=0).astype(jnp.bfloat16)
        return 0

    lax.fori_loop(0, chunks, chunk, 0)
    proj_ref[...] = acc_ref[...].astype(jnp.bfloat16)
    lanes = lax.broadcasted_iota(jnp.int32, (1, chunks * cells), 1)
    pick = (ccol_ref[...] == lanes).astype(jnp.float32).astype(jnp.bfloat16)
    pick_in = (ccol_in_ref[...] == lanes).astype(jnp.float32).astype(jnp.bfloat16)
    step = 512
    for s in range(flat // step):
        part = gc_ref[:, s * step : (s + 1) * step]
        gw_ref[:, s * step : (s + 1) * step] = mm(pick, part).astype(jnp.bfloat16)
        gw_in_ref[:, s * step : (s + 1) * step] = mm(pick_in, part).astype(jnp.bfloat16)


def dense_call(tok_all, up, weights, w_in, cell, cell_in):
    d_count, tok_count, feat = tok_all.shape
    cols = up.shape[1]
    span = GROUP * BLOCK
    cells = GROUP * (cols // BLOCK)
    chunks = d_count * feat // span
    flat = BLOCK * BLOCK
    nb, ns = weights.shape[0], w_in.shape[0]
    vm = pl.BlockSpec(memory_space=pltpu.VMEM)
    return pl.pallas_call(
        dense_kernel,
        out_shape=(
            jax.ShapeDtypeStruct((tok_count, cols), jnp.bfloat16),
            jax.ShapeDtypeStruct((d_count, tok_count, feat), jnp.bfloat16),
            jax.ShapeDtypeStruct((nb, flat), jnp.bfloat16),
            jax.ShapeDtypeStruct((ns, flat), jnp.bfloat16),
        ),
        in_specs=[vm] * 8,
        out_specs=(vm,) * 4,
        scratch_shapes=[
            pltpu.VMEM((cells, flat), jnp.float32),
            pltpu.VMEM((span, cols), jnp.bfloat16),
            pltpu.VMEM((chunks * cells, flat), jnp.bfloat16),
            pltpu.VMEM((span, cols), jnp.float32),
            pltpu.VMEM((tok_count, cols), jnp.float32),
        ],
        compiler_params=pltpu.CompilerParams(vmem_limit_bytes=48 * 1024 * 1024),
        name="dense",
    )(tok_all, up, weights, w_in, cell[None, :], cell_in[None, :], cell[:, None], cell_in[:, None])


def cell_of(row, col):
    return (row // GROUP) * (GROUP * GROUP) + col * GROUP + row % GROUP


def plan(block_rows, block_cols, col_blocks, model_count, my_index):
    nb = block_rows.shape[0]
    target = block_cols // col_blocks
    home = target == my_index
    entry = jnp.arange(nb)
    earlier = (entry[None, :] < entry[:, None]) & (target[None, :] == target[:, None])
    rank = jnp.sum(earlier.astype(jnp.int32), axis=1)
    slot = jnp.where(home, -1, target * CAP + rank)
    local_col = block_cols % col_blocks
    return home, slot, local_col


def per_device(tokens, weight_blocks, block_rows, block_cols, importance, cotangent):
    tok_count = tokens.shape[0]
    model_count = lax.axis_size("mp")
    data_count = lax.axis_size("dp")
    my_index = lax.axis_index("mp")
    col_blocks = cotangent.shape[1] // BLOCK
    slots = model_count * CAP
    flat = BLOCK * BLOCK
    grad_scale = 1.0 / math.sqrt(tok_count * data_count)
    gathered = lax.all_gather(tokens, "mp", axis=0)
    home, slot, local_col = plan(block_rows, block_cols, col_blocks, model_count, my_index)
    send_hot = (jnp.arange(slots)[:, None] == slot[None, :])
    hot16 = send_hot.astype(jnp.bfloat16)
    payload = jnp.dot(hot16, weight_blocks, preferred_element_type=jnp.float32).astype(jnp.bfloat16)
    used = jnp.sum(send_hot * (local_col + 1)[None, :], axis=1)
    rows = jnp.sum(send_hot * block_rows[None, :], axis=1)
    meta = jnp.stack([rows, used], axis=1).astype(jnp.bfloat16)
    meta = jnp.pad(meta, ((0, 0), (0, 126)))
    payload = jnp.concatenate([payload, meta], axis=1).reshape(model_count, CAP, flat + 128)
    arrived = lax.all_to_all(payload, "mp", split_axis=0, concat_axis=0, tiled=True)
    arrived = arrived.reshape(slots, flat + 128)
    w_in = arrived[:, :flat]
    row_in = arrived[:, flat].astype(jnp.int32)
    col_in = arrived[:, flat + 1].astype(jnp.int32) - 1
    cell = jnp.where(home, cell_of(block_rows, local_col), -1)
    cell_in = jnp.where(col_in >= 0, cell_of(row_in, col_in), -1)
    weighted = importance.astype(jnp.float32) / 64.0
    up = (cotangent.astype(jnp.float32) * weighted[:, None]).astype(jnp.bfloat16)
    projected, gi_parts, gw, gw_in = dense_call(gathered, up, weight_blocks, w_in, cell, cell_in)
    returned = lax.all_to_all(
        gw_in.reshape(model_count, CAP, flat), "mp", split_axis=0, concat_axis=0, tiled=True
    ).reshape(slots, flat)
    back = lax.dot_general(
        hot16, returned, (((0,), (0,)), ((), ())), preferred_element_type=jnp.float32
    ).astype(jnp.bfloat16)
    gw = jnp.where(home[:, None], gw, back)
    weight_sum = lax.psum(gw, "dp").astype(jnp.float32)
    grad_weight = (weight_sum * grad_scale).astype(jnp.bfloat16)
    grad_input = lax.psum_scatter(gi_parts, "mp", scatter_dimension=0, tiled=False)
    return (projected, grad_input, grad_weight)


def solution(mesh):
    return jax.shard_map(
        per_device,
        mesh=mesh,
        in_specs=(P("dp", "mp"), P("mp", None), P("mp"), P("mp"), P("dp"), P("dp", "mp")),
        out_specs=(P("dp", "mp"), P("dp", "mp"), P("mp", None)),
        check_vma=False,
    )
```

time: 292 us -> 210 us (0.72)
  matrix products: 107 us -> 4.05 us
  waiting for transfers between devices: 77.1 us -> 150 us
  local copies, waits for them, and re-layouts: 57.1 us -> 1.52 us
  Pallas kernels: 0 us -> 19.7 us
  other arithmetic: 22 us -> 5.57 us
  blocking collectives: 0 us -> 9.45 us
  starting transfers between devices: 12.6 us -> 5.32 us
    dot_general x29 -> x2, matrix products: 107 us -> 4.05 us  [the longest x1 2.07 us: per_device(): lax.dot_general(hot16, returned, (((0,), (0,)), ((), ())), preferred_elem...]
    psum x1, waiting for transfers between devices: 12.3 us -> 84.6 us  [per_device(): weight_sum = lax.psum(gw, 'dp').astype(jnp.float32)]
    pallas_call x0 -> x1, Pallas kernels: none -> 19.7 us  [dense_call(): pl.pallas_call(dense_kernel, out_shape=(jax.ShapeDtypeStruct((tok_count,...]
    gather x7 -> x0, local copies, waits for them, and re-layouts: 17.7 us -> none  [the longest x1 10.3 us: per_device(): token_taken = jnp.take(token_blocks, block_rows, axis=0)]
    all_to_all x3 -> x1, waiting for transfers between devices: 24.7 us -> 8.32 us  [per_device(): lax.all_to_all(payload, 'mp', split_axis=0, concat_axis=0, tiled=True)]
    all_gather x1, waiting for transfers between devices: 0.02 us -> 14.7 us  [per_device(): gathered = lax.all_gather(tokens, 'mp', axis=0)]
    select_n x13 -> x3, other arithmetic: 11 us -> 0.73 us  [the longest x1 0.71 us: per_device(): cell = jnp.where(home, cell_of(block_rows, local_col), -1)]
    all_to_all x0 -> x1, blocking collectives: none -> 9.45 us  [per_device(): lax.all_to_all(gw_in.reshape(model_count, CAP, flat), 'mp', split_axis=0,...]
  transfers between devices with their start and end apart: 6 -> 4, of which waited for: 5 -> 4; matrix products, arithmetic and copies ran while one was open for 27% -> 4% of each run, Pallas kernels for 0% -> 0%
where the time goes in v1:
time: 210 us; the launch traced here: 209 us
  waiting for transfers between devices  150 us (71%)
  Pallas kernels  19.7 us (9%)
  between operations  13.9 us (7%)
  blocking collectives  9.45 us (4%)
  other arithmetic  5.57 us (3%)
  starting transfers between devices  5.32 us (3%)
  matrix products  4.05 us (2%)
    psum x1, waiting for transfers between devices, per_device(): weight_sum = lax.psum(gw, 'dp').astype(jnp.float32)  84.6 us
    reduce_scatter x1, waiting for transfers between devices, per_device(): lax.psum_scatter(gi_parts, 'mp', scatter_dimension=0, tiled=False)  40.7 us
    pallas_call x1, Pallas kernels, dense_call(): pl.pallas_call(dense_kernel, out_shape=(jax.ShapeDtypeStruct((tok_count,...  19.7 us
    all_gather x1, waiting for transfers between devices, per_device(): gathered = lax.all_gather(tokens, 'mp', axis=0)  14.7 us
    all_to_all x1, blocking collectives, per_device(): lax.all_to_all(gw_in.reshape(model_count, CAP, flat), 'mp', split_axis=0,...  9.45 us
    all_to_all x1, waiting for transfers between devices, per_device(): lax.all_to_all(payload, 'mp', split_axis=0, concat_axis=0, tiled=True)  8.32 us
    all_to_all x1, starting transfers between devices, per_device(): lax.all_to_all(payload, 'mp', split_axis=0, concat_axis=0, tiled=True)  5.2 us
  transfers between devices with their start and end apart: 4, of which 4 were waited for; matrix products, arithmetic and copies ran while one was open for 4% of the time, Pallas kernels for 0%

profile of v1, /device:TPU:0, one launch (start us, length us, event | category | flops | bytes accessed | tf_op | source)
XLA Modules:
  0.0 209.3 jit_solution(5111193777652441333)
XLA Ops:
  7.2 0.0 copy-start.1
  7.2 0.0 copy-start
  7.2 0.0 all-gather.3.cloned.1.call-start
  7.2 0.7 all-gather.3.cloned.1.call-update
  7.9 0.7 fusion.20
  8.6 0.2 convert_reduce_fusion
  8.8 0.8 select_reduce_fusion.1
  9.7 0.1 copy.16
  9.8 2.0 convolution_convert_fusion.1
  11.8 0.8 reshape.139
  12.6 5.2 %all-to-all-start = ((bf16[8,3,4224]{2,1,0:T(4,128)(2,1)}), bf16[8,3,4224]{2,1,0:T(4,128)(2,1)S(1)}, u32[]{:S(2)}, u32[]{:S(2)}) async-start(bf16[8,3,4224]{2,1,0:T(4,128)(2,1)} %reshape.139), calls=%async_computation | async-start | bytes 540672 | tf_op jit(solution)/shard_map/all_to_all | solution.py:162
  17.8 0.0 all-reduce.3.cloned.1.call-start
  17.8 0.1 copy.17.ccol_ref
  18.0 0.0 copy-done.1
  18.0 0.0 copy-done
  18.0 0.1 multiply_convert_fusion.1.up_ref
  18.1 8.3 %all-to-all-done = bf16[8,3,4224]{2,1,0:T(4,128)(2,1)S(1)} async-done(((bf16[8,3,4224]{2,1,0:T(4,128)(2,1)}), bf16[8,3,4224]{2,1,0:T(4,128)(2,1)S(1)}, u32[]{:S(2)}, u32[]{:S(2)}) %all-to-all-start) | async-done | bytes 202784 | tf_op jit(solution)/shard_map/all_to_all | solution.py:162
  26.4 0.2 reshape.140
  26.6 0.2 fusion.18
  26.8 0.2 convert_reduce_fusion.1
  27.0 14.7 %all-gather.3.cloned.1.call-done = bf16[2048,512]{1,0:T(8,128)(2,1)} async-done(((bf16[256,512]{1,0:T(8,128)(2,1)}), bf16[2048,512]{1,0:T(8,128)(2,1)}) %all-gather.3.cloned.1.call-update) | async-done | bytes 2097168 | tf_op jit(solution)/shard_map/all_gather | solution.py:152
  41.7 19.7 %dense.1 = (bf16[256,512]{1,0:T(8,128)(2,1)}, bf16[8,256,512]{2,1,0:T(8,128)(2,1)}, bf16[256,4096]{1,0:T(8,128)(2,1)S(1)}, bf16[24,4096]{1,0:T(8,128)(2,1)S(1)}) custom-call(bf16[8,256,512]{2,1,0:T(8,128)(2,1)} %bitcast.31, bf16[256,512]{1,0:T(8,128)(2,1)S(1)} %multiply_convert_fusion.1.up_ref, bf16[256,4096]{1,0:T(8,128)(2,1)} %w_ref.1, ...), custom_call_target="tpu_custom_call" | custom-call | tf_op jit(solution)/shard_map/dense/pallas_call | solution.py:105
  61.5 0.1 reshape.141
  61.6 9.4 %all_to_all.10 = bf16[8,3,4096]{2,1,0:T(4,128)(2,1)S(1)} all-to-all(bf16[8,3,4096]{2,1,0:T(4,128)(2,1)S(1)} %reshape.141), channel_id=1, replica_groups=mesh['dp'=4,'mp'=8] {'mp'}, dimensions={0} | all-to-all | bytes 393216 | tf_op jit(solution)/shard_map/all_to_all | solution.py:172
  71.1 0.2 reshape.142
  71.2 2.1 fusion
  73.3 0.0 all-reduce.3.cloned.1.call-update
  73.3 0.0 reduce-scatter.2.cloned.1.call-start
  73.4 0.7 reduce-scatter.2.cloned.1.call-update
  74.1 84.6 %all-reduce.3.cloned.1.call-done = bf16[256,4096]{1,0:T(8,128)(2,1)} async-done(((bf16[256,4096]{1,0:T(8,128)(2,1)}), bf16[256,4096]{1,0:T(8,128)(2,1)}) %all-reduce.3.cloned.1.call-update) | async-done | bytes 2097168 | tf_op jit(solution)/shard_map/psum | solution.py:179
  158.7 3.3 %multiply_convert_fusion = bf16[256,4096]{1,0:T(8,128)(2,1)} fusion(bf16[256,4096]{1,0:T(8,128)(2,1)} %all-reduce.3.cloned.1.call-done), kind=kLoop, calls=%fused_computation.3 | loop fusion | flops 3145728 | bytes 4194304 | tf_op jit(solution)/shard_map/convert_element_type | solution.py:180
  162.0 40.7 %reduce-scatter.2.cloned.1.call-done = bf16[1,256,512]{2,1,0:T(8,128)(2,1)} async-done(((bf16[8,256,512]{2,1,0:T(8,128)(2,1)}), bf16[1,256,512]{2,1,0:T(8,128)(2,1)}) %reduce-scatter.2.cloned.1.call-update) | async-done | bytes 262160 | tf_op jit(solution)/shard_map/reduce_scatter | solution.py:181
  (7 shorter events, 0.1 us)
Async XLA Ops:
  7.2 10.8 %copy-start.1 = (s32[256]{0:T(256)S(1)}, s32[256]{0:T(256)}, u32[]{:S(2)}) copy-start(s32[256]{0:T(256)} %param.10) | copy-start | bytes 3076
  7.2 10.8 %copy-start = (bf16[256,512]{1,0:T(8,128)(2,1)S(1)}, bf16[256,512]{1,0:T(8,128)(2,1)}, u32[]{:S(2)}) copy-start(bf16[256,512]{1,0:T(8,128)(2,1)} %param.11) | copy-start | bytes 786436
  7.2 34.6 %all-gather.3.cloned.1.call-start = ((), (), s32[]{:S(2)}) async-start(), calls=%async_computation.5 | async-start | bytes 2359296 | tf_op jit(solution)/shard_map/all_gather | solution.py:152
  12.6 13.9 %all-to-all-start = ((bf16[8,3,4224]{2,1,0:T(4,128)(2,1)}), bf16[8,3,4224]{2,1,0:T(4,128)(2,1)S(1)}, u32[]{:S(2)}, u32[]{:S(2)}) async-start(bf16[8,3,4224]{2,1,0:T(4,128)(2,1)} %reshape.139), calls=%async_computation | async-start | bytes 540672 | tf_op jit(solution)/shard_map/all_to_all | solution.py:162
  17.8 140.9 %all-reduce.3.cloned.1.call-start = ((), (), s32[]{:S(2)}) async-start(), calls=%async_computation.4 | async-start | bytes 4194304 | tf_op jit(solution)/shard_map/psum | solution.py:179
  73.3 129.4 %reduce-scatter.2.cloned.1.call-start = ((), (), s32[]{:S(2)}) async-start(), calls=%async_computation.3 | async-start | bytes 2359296 | tf_op jit(solution)/shard_map/reduce_scatter | solution.py:181
Sparse Core Ops, SparseCore 0:
  9.9 31.8 all-gather.2
  73.4 85.2 all-reduce.2
  162.6 40.1 reduce-scatter.1

commit v2 on v1

--- a/solution.py
+++ b/solution.py
@@ -124,6 +124,248 @@
     )(tok_all, up, weights, w_in, cell[None, :], cell_in[None, :], cell[:, None], cell_in[:, None])
 
 
+MESH = pl.DeviceIdType.MESH
+ROWS = 16
+
+
+def reduce_kernel(scale, gw_ref, gi_ref, gin_ref, hot_ref, gw_out, gi_out,
+                  rbuf, sbuf, gbuf, ret, flatret, tail, tot,
+                  r_send, r_recv, b_send, b_recv, g_send, g_recv, q_send, q_recv):
+    me, z = lax.axis_index("mp"), lax.axis_index("dp")
+    n_mp, n = lax.axis_size("mp"), lax.axis_size("dp")
+    nb, flat = gw_ref.shape
+    half = flat // 2
+    count = nb // ROWS
+    tail_rows = tail.shape[0]
+    cap = gin_ref.shape[1]
+    first_tail = count - tail_rows // ROWS
+    low, high = z > 0, z < n - 1
+
+    barrier = pltpu.get_barrier_semaphore()
+
+    def peer(i):
+        return lax.rem(me + i, n_mp)
+
+    def greet(i, _):
+        pl.semaphore_signal(barrier, inc=1, device_id={"mp": peer(i)}, device_id_type=MESH)
+        return 0
+
+    lax.fori_loop(1, n_mp, greet, 0)
+
+    @pl.when(low)
+    def _():
+        pl.semaphore_signal(barrier, inc=1, device_id={"dp": z - 1}, device_id_type=MESH)
+
+    @pl.when(high)
+    def _():
+        pl.semaphore_signal(barrier, inc=1, device_id={"dp": z + 1}, device_id_type=MESH)
+
+    pl.semaphore_wait(barrier, n_mp - 1 + low.astype(jnp.int32) + high.astype(jnp.int32))
+
+    def back_copy(i, into):
+        d = peer(i)
+        return pltpu.make_async_remote_copy(
+            src_ref=gin_ref.at[d], dst_ref=ret.at[me if into is None else into],
+            send_sem=q_send.at[d], recv_sem=q_recv.at[me if into is None else into],
+            device_id={"mp": d}, device_id_type=MESH)
+
+    def gi_copy(i, into):
+        d = peer(i)
+        return pltpu.make_async_remote_copy(
+            src_ref=gi_ref.at[d], dst_ref=gbuf.at[me if into is None else into],
+            send_sem=g_send.at[d], recv_sem=g_recv.at[me if into is None else into],
+            device_id={"mp": d}, device_id_type=MESH)
+
+    def start_back(i, _):
+        back_copy(i, None).start()
+        return 0
+
+    def start_gi(i, _):
+        gi_copy(i, None).start()
+        return 0
+
+    lax.fori_loop(1, n_mp, start_back, 0)
+    lax.fori_loop(1, n_mp, start_gi, 0)
+    ret[me] = jnp.zeros(ret.shape[1:], ret.dtype)
+
+    def rows_of(c):
+        return pl.ds(pl.multiple_of(c * ROWS, ROWS), ROWS)
+
+    def lanes_of(h):
+        return slice(h * half, (h + 1) * half)
+
+    def chain(h, side, c):
+        target = z + 1 if side == 0 else z - 1
+        return pltpu.make_async_remote_copy(
+            src_ref=sbuf.at[h, rows_of(c)], dst_ref=rbuf.at[h, side, rows_of(c)],
+            send_sem=r_send.at[h, c], recv_sem=r_recv.at[h, side, c],
+            device_id={"dp": target}, device_id_type=MESH)
+
+    def spread(h, side, c):
+        target = z + 1 if side == 0 else z - 1
+        return pltpu.make_async_remote_copy(
+            src_ref=gw_out.at[rows_of(c), lanes_of(h)], dst_ref=gw_out.at[rows_of(c), lanes_of(h)],
+            send_sem=b_send.at[h, side, c], recv_sem=b_recv.at[h, c],
+            device_id={"dp": target}, device_id_type=MESH)
+
+    def send_out(h, c, root):
+        @pl.when(low & (z <= root))
+        def _():
+            spread(h, 1, c).start()
+
+        @pl.when(high & (z >= root))
+        def _():
+            spread(h, 0, c).start()
+
+    def gather_in(own_ref, offset, c):
+        for h in range(2):
+            root = n // 2 - h
+            tot[...] = own_ref[rows_of(c - offset), lanes_of(h)].astype(jnp.float32)
+
+            @pl.when(low & (z <= root))
+            def _():
+                chain(h, 0, c).wait_recv()
+                tot[...] += rbuf[h, 0, rows_of(c)].astype(jnp.float32)
+
+            @pl.when(high & (z >= root))
+            def _():
+                chain(h, 1, c).wait_recv()
+                tot[...] += rbuf[h, 1, rows_of(c)].astype(jnp.float32)
+
+            @pl.when(z == root)
+            def _():
+                gw_out[rows_of(c), lanes_of(h)] = (tot[...] * scale).astype(jnp.bfloat16)
+                send_out(h, c, root)
+
+            @pl.when(z != root)
+            def _():
+                sbuf[h, rows_of(c)] = tot[...].astype(jnp.bfloat16)
+
+            @pl.when(z < root)
+            def _():
+                chain(h, 0, c).start()
+
+            @pl.when(z > root)
+            def _():
+                chain(h, 1, c).start()
+
+    def pass_out(c):
+        for h in range(2):
+            root = n // 2 - h
+
+            @pl.when(z != root)
+            def _():
+                spread(h, 0, c).wait_recv()
+                send_out(h, c, root)
+
+    lag = n
+
+    def body(own_ref, offset):
+        def step(s, _):
+            gather_in(own_ref, offset, s)
+
+            @pl.when(s >= lag)
+            def _():
+                pass_out(s - lag)
+
+            return 0
+
+        return step
+
+    lax.fori_loop(0, first_tail, body(gw_ref, 0), 0)
+
+    def wait_back(i, _):
+        back_copy(i, peer(i)).wait_recv()
+        return 0
+
+    lax.fori_loop(1, n_mp, wait_back, 0)
+    for d in range(n_mp):
+        flatret[d * cap : (d + 1) * cap, :] = ret[d].astype(jnp.float32)
+    start = first_tail * ROWS
+    tail[...] = (
+        gw_ref[start:nb, :].astype(jnp.float32)
+        + mm(hot_ref[...], flatret[...].astype(jnp.bfloat16))
+    ).astype(jnp.bfloat16)
+    lax.fori_loop(first_tail, count, body(tail, first_tail), 0)
+
+    def drain(s, _):
+        pass_out(s)
+        return 0
+
+    lax.fori_loop(max(count - lag, 0), count, drain, 0)
+
+    def finish(i, _):
+        gi_copy(i, peer(i)).wait_recv()
+        return 0
+
+    lax.fori_loop(1, n_mp, finish, 0)
+    total = gi_ref[me].astype(jnp.float32)
+    gbuf[me] = jnp.zeros(gbuf.shape[1:], gbuf.dtype)
+    for d in range(n_mp):
+        total = total + gbuf[d].astype(jnp.float32)
+    gi_out[...] = total.astype(jnp.bfloat16)
+
+    def sent(i, _):
+        back_copy(i, None).wait_send()
+        gi_copy(i, None).wait_send()
+        return 0
+
+    lax.fori_loop(1, n_mp, sent, 0)
+
+    def sent_z(c, _):
+        for h in range(2):
+            root = n // 2 - h
+
+            @pl.when(z != root)
+            def _():
+                chain(h, 0, c).wait_send()
+
+            @pl.when(low & (z <= root))
+            def _():
+                spread(h, 1, c).wait_send()
+
+            @pl.when(high & (z >= root))
+            def _():
+                spread(h, 0, c).wait_send()
+
+        return 0
+
+    lax.fori_loop(0, count, sent_z, 0)
+
+
+def reduce_call(gw, gi_parts, gw_in, hot_tail, scale, data_count):
+    nb, flat = gw.shape
+    n_mp, tok_count, feat = gi_parts.shape
+    count, half = nb // ROWS, flat // 2
+    cap = gw_in.shape[1]
+    dma = pltpu.SemaphoreType.DMA
+    vm = pl.BlockSpec(memory_space=pltpu.VMEM)
+    return pl.pallas_call(
+        functools.partial(reduce_kernel, scale),
+        out_shape=(
+            jax.ShapeDtypeStruct((nb, flat), jnp.bfloat16),
+            jax.ShapeDtypeStruct((tok_count, feat), jnp.bfloat16),
+        ),
+        in_specs=[vm] * 4,
+        out_specs=(vm,) * 2,
+        scratch_shapes=[
+            pltpu.VMEM((2, 2, nb, half), jnp.bfloat16),
+            pltpu.VMEM((2, nb, half), jnp.bfloat16),
+            pltpu.VMEM(gi_parts.shape, jnp.bfloat16),
+            pltpu.VMEM(gw_in.shape, jnp.bfloat16),
+            pltpu.VMEM((n_mp * cap, flat), jnp.float32),
+            pltpu.VMEM((hot_tail.shape[0], flat), jnp.bfloat16),
+            pltpu.VMEM((ROWS, half), jnp.float32),
+            dma((2, count)), dma((2, 2, count)), dma((2, 2, count)), dma((2, count)),
+            dma((n_mp,)), dma((n_mp,)), dma((n_mp,)), dma((n_mp,)),
+        ],
+        compiler_params=pltpu.CompilerParams(
+            collective_id=0, has_side_effects=True, vmem_limit_bytes=48 * 1024 * 1024
+        ),
+        name="reduce",
+    )(gw, gi_parts, gw_in, hot_tail)
+
+
 def cell_of(row, col):
     return (row // GROUP) * (GROUP * GROUP) + col * GROUP + row % GROUP
 
@@ -169,16 +411,11 @@
     weighted = importance.astype(jnp.float32) / 64.0
     up = (cotangent.astype(jnp.float32) * weighted[:, None]).astype(jnp.bfloat16)
     projected, gi_parts, gw, gw_in = dense_call(gathered, up, weight_blocks, w_in, cell, cell_in)
-    returned = lax.all_to_all(
-        gw_in.reshape(model_count, CAP, flat), "mp", split_axis=0, concat_axis=0, tiled=True
-    ).reshape(slots, flat)
-    back = lax.dot_general(
-        hot16, returned, (((0,), (0,)), ((), ())), preferred_element_type=jnp.float32
-    ).astype(jnp.bfloat16)
-    gw = jnp.where(home[:, None], gw, back)
-    weight_sum = lax.psum(gw, "dp").astype(jnp.float32)
-    grad_weight = (weight_sum * grad_scale).astype(jnp.bfloat16)
-    grad_input = lax.psum_scatter(gi_parts, "mp", scatter_dimension=0, tiled=False)
+    tail_rows = min(-(-slots // ROWS) * ROWS, block_rows.shape[0])
+    hot_tail = hot16.T[block_rows.shape[0] - tail_rows :]
+    grad_weight, grad_input = reduce_call(
+        gw, gi_parts, gw_in.reshape(model_count, CAP, flat), hot_tail, grad_scale, data_count
+    )
     return (projected, grad_input, grad_weight)
 
 

time: 210 us -> 300 us (1.43)
  Pallas kernels: 19.7 us -> 247 us
  waiting for transfers between devices: 150 us -> 23.6 us
  blocking collectives: 9.45 us -> 0 us
  other arithmetic: 5.57 us -> 2.31 us
  local copies, waits for them, and re-layouts: 1.52 us -> 4.78 us
    pallas_call x0 -> x1, Pallas kernels: none -> 227 us  [reduce_call(): pl.pallas_call(functools.partial(reduce_kernel, scale), out_shape=(jax.Sh...]
    psum x1 -> x0, waiting for transfers between devices: 84.6 us -> none  [per_device(): weight_sum = lax.psum(gw, 'dp').astype(jnp.float32)]
    reduce_scatter x1 -> x0, waiting for transfers between devices: 40.7 us -> none  [per_device(): lax.psum_scatter(gi_parts, 'mp', scatter_dimension=0, tiled=False)]
    all_to_all x1 -> x0, blocking collectives: 9.45 us -> none  [per_device(): lax.all_to_all(gw_in.reshape(model_count, CAP, flat), 'mp', split_axis=0,...]
    unnamed x4 -> x8, local copies, waits for them, and re-layouts: 0.01 us -> 3.35 us
    convert_element_type x1 -> x0, other arithmetic: 3.33 us -> none  [per_device(): grad_weight = (weight_sum * grad_scale).astype(jnp.bfloat16)]
  transfers between devices with their start and end apart: 4 -> 2, of which waited for: 4 -> 2; matrix products, arithmetic and copies ran while one was open for 4% -> 2% of each run, Pallas kernels for 0% -> 0%
where the time goes in v2:
time: 300 us; the launch traced here: 299 us
  Pallas kernels  247 us (82%)
  waiting for transfers between devices  23.6 us (8%)
  between operations  14.1 us (5%)
  starting transfers between devices  5.24 us (2%)
  local copies, waits for them, and re-layouts  4.78 us (2%)
    pallas_call x1, Pallas kernels, reduce_call(): pl.pallas_call(functools.partial(reduce_kernel, scale), out_shape=(jax.Sh...  227 us
    pallas_call x1, Pallas kernels, dense_call(): pl.pallas_call(dense_kernel, out_shape=(jax.ShapeDtypeStruct((tok_count,...  19.7 us
    all_gather x1, waiting for transfers between devices, per_device(): gathered = lax.all_gather(tokens, 'mp', axis=0)  14.7 us
    all_to_all x1, waiting for transfers between devices, per_device(): lax.all_to_all(payload, 'mp', split_axis=0, concat_axis=0, tiled=True)  8.22 us
  transfers between devices with their start and end apart: 2, of which 2 were waited for; matrix products, arithmetic and copies ran while one was open for 2% of the time, Pallas kernels for 0%

profile of v2, /device:TPU:0, one launch (start us, length us, event | category | flops | bytes accessed | tf_op | source)
XLA Modules:
  0.0 299.2 jit_solution(7492682646749641873)
XLA Ops:
  7.2 0.0 copy-start.2
  7.2 0.0 copy-start.1
  7.2 0.0 all-gather.3.cloned.1.call-start
  7.2 0.7 all-gather.3.cloned.1.call-update
  7.9 0.7 fusion.19
  8.6 0.2 convert_reduce_fusion
  8.8 0.8 select_reduce_fusion.1
  9.7 0.1 copy.16
  9.8 2.0 convolution_convert_fusion
  11.8 0.8 reshape.135
  12.6 5.2 %all-to-all-start = ((bf16[8,3,4224]{2,1,0:T(4,128)(2,1)}), bf16[8,3,4224]{2,1,0:T(4,128)(2,1)S(1)}, u32[]{:S(2)}, u32[]{:S(2)}) async-start(bf16[8,3,4224]{2,1,0:T(4,128)(2,1)} %reshape.135), calls=%async_computation | async-start | bytes 540672 | tf_op jit(solution)/shard_map/all_to_all | solution.py:404
  17.8 0.1 slice.22
  17.8 0.1 copy.17.ccol_ref
  18.0 0.0 copy-done.2
  18.0 0.0 copy-done.1
  18.0 0.1 multiply_convert_fusion.up_ref
  18.1 0.1 fusion.3.hot_ref
  18.2 8.2 %all-to-all-done = bf16[8,3,4224]{2,1,0:T(4,128)(2,1)S(1)} async-done(((bf16[8,3,4224]{2,1,0:T(4,128)(2,1)}), bf16[8,3,4224]{2,1,0:T(4,128)(2,1)S(1)}, u32[]{:S(2)}, u32[]{:S(2)}) %all-to-all-start) | async-done | bytes 202784 | tf_op jit(solution)/shard_map/all_to_all | solution.py:404
  26.4 0.2 reshape.136
  26.6 0.2 fusion.17
  26.8 0.2 convert_reduce_fusion.1
  27.0 14.7 %all-gather.3.cloned.1.call-done = bf16[2048,512]{1,0:T(8,128)(2,1)} async-done(((bf16[256,512]{1,0:T(8,128)(2,1)}), bf16[2048,512]{1,0:T(8,128)(2,1)}) %all-gather.3.cloned.1.call-update) | async-done | bytes 2097168 | tf_op jit(solution)/shard_map/all_gather | solution.py:394
  41.7 19.7 %dense.1 = (bf16[256,512]{1,0:T(8,128)(2,1)}, bf16[8,256,512]{2,1,0:T(8,128)(2,1)S(1)}, bf16[256,4096]{1,0:T(8,128)(2,1)S(1)}, bf16[24,4096]{1,0:T(8,128)(2,1)S(1)}) custom-call(bf16[8,256,512]{2,1,0:T(8,128)(2,1)} %bitcast.29, bf16[256,512]{1,0:T(8,128)(2,1)S(1)} %multiply_convert_fusion.up_ref, bf16[256,4096]{1,0:T(8,128)(2,1)} %w_ref.1, ...), custom_call_target="tpu_custom_call" | custom-call | tf_op jit(solution)/shard_map/dense/pallas_call | solution.py:105
  61.4 0.0 copy-start
  61.4 1.3 copy-done
  62.7 0.1 reshape.137.gin_ref
  62.8 227.5 %reduce.7 = (bf16[256,4096]{1,0:T(8,128)(2,1)S(1)}, bf16[256,512]{1,0:T(8,128)(2,1)S(1)}) custom-call(bf16[256,4096]{1,0:T(8,128)(2,1)S(1)} %get-tuple-element.10.gw_ref, bf16[8,256,512]{2,1,0:T(8,128)(2,1)} %copy-done, bf16[8,3,4096]{2,1,0:T(4,128)(2,1)S(1)} %reshape.137.gin_ref, bf16[32,24]{1,0:T(8,128)(2,1)S(1)} %fusion.3.hot_ref), custom_call_target="tpu_custom_call" | custom-call | tf_op jit(solution)/shard_map/reduce/pallas_call | solution.py:343
  290.3 0.7 copy.20
  291.0 1.3 copy.21
  (7 shorter events, 0.1 us)
Async XLA Ops:
  7.2 10.8 %copy-start.2 = (s32[256]{0:T(256)S(1)}, s32[256]{0:T(256)}, u32[]{:S(2)}) copy-start(s32[256]{0:T(256)} %param.10) | copy-start | bytes 3076
  7.2 10.8 %copy-start.1 = (bf16[256,512]{1,0:T(8,128)(2,1)S(1)}, bf16[256,512]{1,0:T(8,128)(2,1)}, u32[]{:S(2)}) copy-start(bf16[256,512]{1,0:T(8,128)(2,1)} %param.11) | copy-start | bytes 786436
  7.2 34.5 %all-gather.3.cloned.1.call-start = ((), (), s32[]{:S(2)}) async-start(), calls=%async_computation.1 | async-start | bytes 2359296 | tf_op jit(solution)/shard_map/all_gather | solution.py:394
  12.6 13.9 %all-to-all-start = ((bf16[8,3,4224]{2,1,0:T(4,128)(2,1)}), bf16[8,3,4224]{2,1,0:T(4,128)(2,1)S(1)}, u32[]{:S(2)}, u32[]{:S(2)}) async-start(bf16[8,3,4224]{2,1,0:T(4,128)(2,1)} %reshape.135), calls=%async_computation | async-start | bytes 540672 | tf_op jit(solution)/shard_map/all_to_all | solution.py:404
  61.4 1.3 copy-start
Sparse Core Ops, SparseCore 0:
  9.9 31.8 all-gather.2

commit v3 on v2

--- a/solution.py
+++ b/solution.py
@@ -126,6 +126,7 @@
 
 MESH = pl.DeviceIdType.MESH
 ROWS = 16
+SLACK = 2
 
 
 def reduce_kernel(scale, gw_ref, gi_ref, gin_ref, hot_ref, gw_out, gi_out,
@@ -217,62 +218,64 @@
         def _():
             spread(h, 0, c).start()
 
-    def gather_in(own_ref, offset, c):
+    def gather_in(h, root, c):
+        @pl.when(c < first_tail)
+        def _():
+            tot[...] = gw_ref[rows_of(c), lanes_of(h)].astype(jnp.float32)
+
+        @pl.when(c >= first_tail)
+        def _():
+            tot[...] = tail[rows_of(c - first_tail), lanes_of(h)].astype(jnp.float32)
+
+        @pl.when(low & (z <= root))
+        def _():
+            chain(h, 0, c).wait_recv()
+            tot[...] += rbuf[h, 0, rows_of(c)].astype(jnp.float32)
+
+        @pl.when(high & (z >= root))
+        def _():
+            chain(h, 1, c).wait_recv()
+            tot[...] += rbuf[h, 1, rows_of(c)].astype(jnp.float32)
+
+        @pl.when(z == root)
+        def _():
+            gw_out[rows_of(c), lanes_of(h)] = (tot[...] * scale).astype(jnp.bfloat16)
+            send_out(h, c, root)
+
+        @pl.when(z != root)
+        def _():
+            sbuf[h, rows_of(c)] = tot[...].astype(jnp.bfloat16)
+
+        @pl.when(z < root)
+        def _():
+            chain(h, 0, c).start()
+
+        @pl.when(z > root)
+        def _():
+            chain(h, 1, c).start()
+
+    far = n // 2
+
+    def step(s, _):
         for h in range(2):
             root = n // 2 - h
-            tot[...] = own_ref[rows_of(c - offset), lanes_of(h)].astype(jnp.float32)
-
-            @pl.when(low & (z <= root))
+            away = jnp.where(z < root, root - z, z - root)
+            c = s - SLACK * (far - away)
+
+            @pl.when((c >= 0) & (c < count))
             def _():
-                chain(h, 0, c).wait_recv()
-                tot[...] += rbuf[h, 0, rows_of(c)].astype(jnp.float32)
-
-            @pl.when(high & (z >= root))
+                gather_in(h, root, c)
+
+            late = s - SLACK * (far + away)
+
+            @pl.when((late >= 0) & (late < count) & (z != root))
             def _():
-                chain(h, 1, c).wait_recv()
-                tot[...] += rbuf[h, 1, rows_of(c)].astype(jnp.float32)
-
-            @pl.when(z == root)
-            def _():
-                gw_out[rows_of(c), lanes_of(h)] = (tot[...] * scale).astype(jnp.bfloat16)
-                send_out(h, c, root)
-
-            @pl.when(z != root)
-            def _():
-                sbuf[h, rows_of(c)] = tot[...].astype(jnp.bfloat16)
-
-            @pl.when(z < root)
-            def _():
-                chain(h, 0, c).start()
-
-            @pl.when(z > root)
-            def _():
-                chain(h, 1, c).start()
-
-    def pass_out(c):
-        for h in range(2):
-            root = n // 2 - h
-
-            @pl.when(z != root)
-            def _():
-                spread(h, 0, c).wait_recv()
-                send_out(h, c, root)
-
-    lag = n
-
-    def body(own_ref, offset):
-        def step(s, _):
-            gather_in(own_ref, offset, s)
-
-            @pl.when(s >= lag)
-            def _():
-                pass_out(s - lag)
-
-            return 0
-
-        return step
-
-    lax.fori_loop(0, first_tail, body(gw_ref, 0), 0)
+                spread(h, 0, late).wait_recv()
+                send_out(h, late, root)
+
+        return 0
+
+    lax.fori_loop(0, first_tail, step, 0)
 
     def wait_back(i, _):
         back_copy(i, peer(i)).wait_recv()
@@ -286,13 +289,7 @@
         gw_ref[start:nb, :].astype(jnp.float32)
         + mm(hot_ref[...], flatret[...].astype(jnp.bfloat16))
     ).astype(jnp.bfloat16)
-    lax.fori_loop(first_tail, count, body(tail, first_tail), 0)
-
-    def drain(s, _):
-        pass_out(s)
-        return 0
-
-    lax.fori_loop(max(count - lag, 0), count, drain, 0)
+    lax.fori_loop(first_tail, count + 2 * SLACK * far, step, 0)
 
     def finish(i, _):
         gi_copy(i, peer(i)).wait_recv()

time: 300 us -> 134 us (0.45)
  Pallas kernels: 247 us -> 81.8 us
    pallas_call x1, Pallas kernels: 227 us -> 62.1 us  [reduce_call(): pl.pallas_call(functools.partial(reduce_kernel, scale), out_shape=(jax.Sh...]
  transfers between devices with their start and end apart: 2 -> 2, of which waited for: 2 -> 2; matrix products, arithmetic and copies ran while one was open for 2% -> 4% of each run, Pallas kernels for 0% -> 0%
where the time goes in v3:
time: 134 us
  Pallas kernels  81.8 us (61%)
  waiting for transfers between devices  23.6 us (18%)
  between operations  14.1 us (11%)
  starting transfers between devices  5.24 us (4%)
  local copies, waits for them, and re-layouts  4.78 us (4%)
  other arithmetic  2.31 us (2%)
  matrix products  1.98 us (1%)
    pallas_call x1, Pallas kernels, reduce_call(): pl.pallas_call(functools.partial(reduce_kernel, scale), out_shape=(jax.Sh...  62.1 us
    pallas_call x1, Pallas kernels, dense_call(): pl.pallas_call(dense_kernel, out_shape=(jax.ShapeDtypeStruct((tok_count,...  19.7 us
    all_gather x1, waiting for transfers between devices, per_device(): gathered = lax.all_gather(tokens, 'mp', axis=0)  14.7 us
    all_to_all x1, waiting for transfers between devices, per_device(): lax.all_to_all(payload, 'mp', split_axis=0, concat_axis=0, tiled=True)  8.22 us
    all_to_all x1, starting transfers between devices, per_device(): lax.all_to_all(payload, 'mp', split_axis=0, concat_axis=0, tiled=True)  5.2 us
    unnamed x8, local copies, waits for them, and re-layouts  3.35 us
  transfers between devices with their start and end apart: 2, of which 2 were waited for; matrix products, arithmetic and copies ran while one was open for 4% of the time, Pallas kernels for 0%

profile of v3, /device:TPU:0, one launch (start us, length us, event | category | flops | bytes accessed | tf_op | source)
XLA Modules:
  0.0 133.8 jit_solution(12585371970130112922)
XLA Ops:
  7.2 0.0 copy-start.2
  7.2 0.0 copy-start.1
  7.2 0.0 all-gather.3.cloned.1.call-start
  7.2 0.7 all-gather.3.cloned.1.call-update
  7.9 0.7 fusion.19
  8.6 0.2 convert_reduce_fusion
  8.8 0.8 select_reduce_fusion.1
  9.7 0.1 copy.16
  9.8 2.0 %convolution_convert_fusion = bf16[24,4096]{1,0:T(8,128)(2,1)S(1)} fusion(bf16[256,4096]{1,0:T(8,128)(2,1)} %w_ref.1, s32[256]{0:T(256)S(1)} %add_select_fusion.2), kind=kOutput, calls=%fused_computation | convolution fusion | flops 50436096 | bytes 2294784 | tf_op jit(solution)/shard_map/dot_general | solution.py:395
  11.8 0.8 reshape.135
  12.6 5.2 %all-to-all-start = ((bf16[8,3,4224]{2,1,0:T(4,128)(2,1)}), bf16[8,3,4224]{2,1,0:T(4,128)(2,1)S(1)}, u32[]{:S(2)}, u32[]{:S(2)}) async-start(bf16[8,3,4224]{2,1,0:T(4,128)(2,1)} %reshape.135), calls=%async_computation | async-start | bytes 540672 | tf_op jit(solution)/shard_map/all_to_all | solution.py:401
  17.8 0.1 slice.22
  17.8 0.1 copy.17.ccol_ref
  18.0 0.0 copy-done.2
  18.0 0.0 copy-done.1
  18.0 0.1 multiply_convert_fusion.up_ref
  18.1 0.1 fusion.3.hot_ref
  18.2 8.2 %all-to-all-done = bf16[8,3,4224]{2,1,0:T(4,128)(2,1)S(1)} async-done(((bf16[8,3,4224]{2,1,0:T(4,128)(2,1)}), bf16[8,3,4224]{2,1,0:T(4,128)(2,1)S(1)}, u32[]{:S(2)}, u32[]{:S(2)}) %all-to-all-start) | async-done | bytes 202784 | tf_op jit(solution)/shard_map/all_to_all | solution.py:401
  26.4 0.2 reshape.136
  26.6 0.2 fusion.17
  26.8 0.2 convert_reduce_fusion.1
  27.0 14.7 %all-gather.3.cloned.1.call-done = bf16[2048,512]{1,0:T(8,128)(2,1)} async-done(((bf16[256,512]{1,0:T(8,128)(2,1)}), bf16[2048,512]{1,0:T(8,128)(2,1)}) %all-gather.3.cloned.1.call-update) | async-done | bytes 2097168 | tf_op jit(solution)/shard_map/all_gather | solution.py:391
  41.7 19.7 %dense.1 = (bf16[256,512]{1,0:T(8,128)(2,1)}, bf16[8,256,512]{2,1,0:T(8,128)(2,1)S(1)}, bf16[256,4096]{1,0:T(8,128)(2,1)S(1)}, bf16[24,4096]{1,0:T(8,128)(2,1)S(1)}) custom-call(bf16[8,256,512]{2,1,0:T(8,128)(2,1)} %bitcast.29, bf16[256,512]{1,0:T(8,128)(2,1)S(1)} %multiply_convert_fusion.up_ref, bf16[256,4096]{1,0:T(8,128)(2,1)} %w_ref.1, ...), custom_call_target="tpu_custom_call" | custom-call | tf_op jit(solution)/shard_map/dense/pallas_call | solution.py:105
  61.4 0.0 copy-start
  61.4 1.3 copy-done
  62.7 0.1 reshape.137.gin_ref
  62.8 62.1 %reduce.7 = (bf16[256,4096]{1,0:T(8,128)(2,1)S(1)}, bf16[256,512]{1,0:T(8,128)(2,1)S(1)}) custom-call(bf16[256,4096]{1,0:T(8,128)(2,1)S(1)} %get-tuple-element.10.gw_ref, bf16[8,256,512]{2,1,0:T(8,128)(2,1)} %copy-done, bf16[8,3,4096]{2,1,0:T(4,128)(2,1)S(1)} %reshape.137.gin_ref, bf16[32,24]{1,0:T(8,128)(2,1)S(1)} %fusion.3.hot_ref), custom_call_target="tpu_custom_call" | custom-call | tf_op jit(solution)/shard_map/reduce/pallas_call | solution.py:340
  125.0 0.7 copy.20
  125.7 1.3 copy.21
  (7 shorter events, 0.1 us)
Async XLA Ops:
  7.2 10.8 %copy-start.2 = (s32[256]{0:T(256)S(1)}, s32[256]{0:T(256)}, u32[]{:S(2)}) copy-start(s32[256]{0:T(256)} %param.10) | copy-start | bytes 3076
  7.2 10.8 %copy-start.1 = (bf16[256,512]{1,0:T(8,128)(2,1)S(1)}, bf16[256,512]{1,0:T(8,128)(2,1)}, u32[]{:S(2)}) copy-start(bf16[256,512]{1,0:T(8,128)(2,1)} %param.11) | copy-start | bytes 786436
  7.2 34.5 %all-gather.3.cloned.1.call-start = ((), (), s32[]{:S(2)}) async-start(), calls=%async_computation.1 | async-start | bytes 2359296 | tf_op jit(solution)/shard_map/all_gather | solution.py:391
  12.6 13.9 %all-to-all-start = ((bf16[8,3,4224]{2,1,0:T(4,128)(2,1)}), bf16[8,3,4224]{2,1,0:T(4,128)(2,1)S(1)}, u32[]{:S(2)}, u32[]{:S(2)}) async-start(bf16[8,3,4224]{2,1,0:T(4,128)(2,1)} %reshape.135), calls=%async_computation | async-start | bytes 540672 | tf_op jit(solution)/shard_map/all_to_all | solution.py:401
  61.4 1.3 copy-start
Sparse Core Ops, SparseCore 0:
  9.9 31.8 all-gather.2

commit v4 on v3

--- a/solution.py
+++ b/solution.py
@@ -363,6 +363,74 @@
     )(gw, gi_parts, gw_in, hot_tail)
 
 
+def gather_kernel(tok_ref, pay_ref, tok_out, pay_out, t_send, t_recv, p_send, p_recv):
+    me, n_mp = lax.axis_index("mp"), lax.axis_size("mp")
+    barrier = pltpu.get_barrier_semaphore()
+
+    def peer(i):
+        return lax.rem(me + i, n_mp)
+
+    def copies(i, slot):
+        d = peer(i)
+        return (
+            pltpu.make_async_remote_copy(
+                src_ref=pay_ref.at[d], dst_ref=pay_out.at[slot],
+                send_sem=p_send.at[d], recv_sem=p_recv.at[slot],
+                device_id={"mp": d}, device_id_type=MESH),
+            pltpu.make_async_remote_copy(
+                src_ref=tok_ref, dst_ref=tok_out.at[slot],
+                send_sem=t_send.at[d], recv_sem=t_recv.at[slot],
+                device_id={"mp": d}, device_id_type=MESH),
+        )
+
+    def greet(i, _):
+        pl.semaphore_signal(barrier, inc=1, device_id={"mp": peer(i)}, device_id_type=MESH)
+        return 0
+
+    def start(i, _):
+        for copy in copies(i, me):
+            copy.start()
+        return 0
+
+    def arrive(i, _):
+        for copy in copies(i, peer(i)):
+            copy.wait_recv()
+        return 0
+
+    def leave(i, _):
+        for copy in copies(i, me):
+            copy.wait_send()
+        return 0
+
+    lax.fori_loop(1, n_mp, greet, 0)
+    pl.semaphore_wait(barrier, n_mp - 1)
+    lax.fori_loop(1, n_mp, start, 0)
+    tok_out[me] = tok_ref[...]
+    pay_out[me] = pay_ref[me]
+    lax.fori_loop(1, n_mp, arrive, 0)
+    lax.fori_loop(1, n_mp, leave, 0)
+
+
+def gather_call(tokens, payload):
+    n_mp = payload.shape[0]
+    dma = pltpu.SemaphoreType.DMA
+    vm = pl.BlockSpec(memory_space=pltpu.VMEM)
+    return pl.pallas_call(
+        gather_kernel,
+        out_shape=(
+            jax.ShapeDtypeStruct((n_mp,) + tokens.shape, jnp.bfloat16),
+            jax.ShapeDtypeStruct(payload.shape, jnp.bfloat16),
+        ),
+        in_specs=[vm] * 2,
+        out_specs=(vm,) * 2,
+        scratch_shapes=[dma((n_mp,))] * 4,
+        compiler_params=pltpu.CompilerParams(
+            collective_id=1, has_side_effects=True, vmem_limit_bytes=32 * 1024 * 1024
+        ),
+        name="gather",
+    )(tokens, payload)
+
+
 def cell_of(row, col):
     return (row // GROUP) * (GROUP * GROUP) + col * GROUP + row % GROUP
 
@@ -388,7 +456,6 @@
     slots = model_count * CAP
     flat = BLOCK * BLOCK
     grad_scale = 1.0 / math.sqrt(tok_count * data_count)
-    gathered = lax.all_gather(tokens, "mp", axis=0)
     home, slot, local_col = plan(block_rows, block_cols, col_blocks, model_count, my_index)
     send_hot = (jnp.arange(slots)[:, None] == slot[None, :])
     hot16 = send_hot.astype(jnp.bfloat16)
@@ -398,7 +465,7 @@
     meta = jnp.stack([rows, used], axis=1).astype(jnp.bfloat16)
     meta = jnp.pad(meta, ((0, 0), (0, 126)))
     payload = jnp.concatenate([payload, meta], axis=1).reshape(model_count, CAP, flat + 128)
-    arrived = lax.all_to_all(payload, "mp", split_axis=0, concat_axis=0, tiled=True)
+    gathered, arrived = gather_call(tokens, payload)
     arrived = arrived.reshape(slots, flat + 128)
     w_in = arrived[:, :flat]
     row_in = arrived[:, flat].astype(jnp.int32)

time: 134 us -> 124 us (0.925)
  Pallas kernels: 81.8 us -> 113 us
  waiting for transfers between devices: 23.6 us -> 0 us
  between operations: 14.1 us -> 0.78 us
  starting transfers between devices: 5.24 us -> 0 us
    pallas_call x0 -> x1, Pallas kernels: none -> 30.1 us  [gather_call(): pl.pallas_call(gather_kernel, out_shape=(jax.ShapeDtypeStruct((n_mp,) + t...]
    all_gather x1 -> x0, waiting for transfers between devices: 14.7 us -> none  [per_device(): gathered = lax.all_gather(tokens, 'mp', axis=0)]
    all_to_all x1 -> x0, waiting for transfers between devices: 8.22 us -> none  [per_device(): lax.all_to_all(payload, 'mp', split_axis=0, concat_axis=0, tiled=True)]
    all_to_all x1 -> x0, starting transfers between devices: 5.2 us -> none  [per_device(): lax.all_to_all(payload, 'mp', split_axis=0, concat_axis=0, tiled=True)]
    pallas_call x1, Pallas kernels: 62.1 us -> 63.5 us  [reduce_call(): pl.pallas_call(functools.partial(reduce_kernel, scale), out_shape=(jax.Sh...]
    unnamed x8 -> x12, local copies, waits for them, and re-layouts: 3.35 us -> 4.67 us
  transfers between devices with their start and end apart: 2 -> 0, of which waited for: 2 -> 0; matrix products, arithmetic and copies ran while one was open for 4% -> 0% of each run, Pallas kernels for 0% -> 0%
where the time goes in v4:
time: 124 us
  Pallas kernels  113 us (91%)
  local copies, waits for them, and re-layouts  5.38 us (4%)
  other arithmetic  2.34 us (2%)
  matrix products  2.02 us (2%)
    pallas_call x1, Pallas kernels, reduce_call(): pl.pallas_call(functools.partial(reduce_kernel, scale), out_shape=(jax.Sh...  63.5 us
    pallas_call x1, Pallas kernels, gather_call(): pl.pallas_call(gather_kernel, out_shape=(jax.ShapeDtypeStruct((n_mp,) + t...  30.1 us
    pallas_call x1, Pallas kernels, dense_call(): pl.pallas_call(dense_kernel, out_shape=(jax.ShapeDtypeStruct((tok_count,...  19.8 us
    unnamed x12, local copies, waits for them, and re-layouts  4.67 us

profile of v4, /device:TPU:0, one launch (start us, length us, event | category | flops | bytes accessed | tf_op | source)
XLA Modules:
  0.0 124.0 jit_solution(10148616618496432783)
XLA Ops:
  0.6 0.0 copy-start.2
  0.6 0.8 fusion.19
  1.4 0.2 convert_reduce_fusion
  1.6 0.8 select_reduce_fusion.1
  2.4 0.1 copy.16
  2.5 0.0 copy-start.4
  2.5 0.0 copy-start.3
  2.5 2.0 %convolution_convert_fusion = bf16[24,4096]{1,0:T(8,128)(2,1)S(1)} fusion(bf16[256,4096]{1,0:T(8,128)(2,1)} %w_ref.1, s32[256]{0:T(256)S(1)} %add_select_fusion.2), kind=kOutput, calls=%fused_computation | convolution fusion | flops 50436096 | bytes 2294784 | tf_op jit(solution)/shard_map/dot_general | solution.py:462
  4.6 0.1 reshape.135.pay_ref
  4.7 0.0 copy-done.2
  4.7 30.1 %gather.1 = (bf16[8,256,512]{2,1,0:T(8,128)(2,1)S(1)}, bf16[8,3,4224]{2,1,0:T(4,128)(2,1)S(1)}) custom-call(bf16[256,512]{1,0:T(8,128)(2,1)S(1)} %copy-done.2, bf16[8,3,4224]{2,1,0:T(4,128)(2,1)S(1)} %reshape.135.pay_ref), custom_call_target="tpu_custom_call" | custom-call | tf_op jit(solution)/shard_map/gather/pallas_call | solution.py:418
  34.8 0.0 copy-start
  34.8 1.3 %copy-done = bf16[8,256,512]{2,1,0:T(8,128)(2,1)} copy-done((bf16[8,256,512]{2,1,0:T(8,128)(2,1)}, bf16[8,256,512]{2,1,0:T(8,128)(2,1)S(1)}, u32[]{:S(2)}) %copy-start) | copy-done | bytes 2097176
  36.2 0.2 reshape.136
  36.3 0.2 convert_reduce_fusion.1
  36.5 0.2 fusion.17
  36.7 0.1 copy.17.ccol_ref
  36.9 0.0 copy-done.4
  36.9 0.0 copy-done.3
  36.9 0.1 multiply_convert_fusion.up_ref
  37.0 19.8 %dense.1 = (bf16[256,512]{1,0:T(8,128)(2,1)}, bf16[8,256,512]{2,1,0:T(8,128)(2,1)S(1)}, bf16[256,4096]{1,0:T(8,128)(2,1)S(1)}, bf16[24,4096]{1,0:T(8,128)(2,1)S(1)}) custom-call(bf16[8,256,512]{2,1,0:T(8,128)(2,1)} %copy-done, bf16[256,512]{1,0:T(8,128)(2,1)S(1)} %multiply_convert_fusion.up_ref, bf16[256,4096]{1,0:T(8,128)(2,1)} %w_ref.1, ...), custom_call_target="tpu_custom_call" | custom-call | tf_op jit(solution)/shard_map/dense/pallas_call | solution.py:105
  56.8 0.0 copy-start.1
  56.8 1.3 %copy-done.1 = bf16[8,256,512]{2,1,0:T(8,128)(2,1)} copy-done((bf16[8,256,512]{2,1,0:T(8,128)(2,1)}, bf16[8,256,512]{2,1,0:T(8,128)(2,1)S(1)}, u32[]{:S(2)}) %copy-start.1) | copy-done | bytes 2097176
  58.2 0.1 reshape.137.gin_ref
  58.3 0.1 slice.22
  58.4 0.1 fusion.3.hot_ref
  58.4 63.5 %reduce.7 = (bf16[256,4096]{1,0:T(8,128)(2,1)S(1)}, bf16[256,512]{1,0:T(8,128)(2,1)S(1)}) custom-call(bf16[256,4096]{1,0:T(8,128)(2,1)S(1)} %get-tuple-element.14.gw_ref, bf16[8,256,512]{2,1,0:T(8,128)(2,1)} %copy-done.1, bf16[8,3,4096]{2,1,0:T(4,128)(2,1)S(1)} %reshape.137.gin_ref, bf16[32,24]{1,0:T(8,128)(2,1)S(1)} %fusion.3.hot_ref), custom_call_target="tpu_custom_call" | custom-call | tf_op jit(solution)/shard_map/reduce/pallas_call | solution.py:340
  122.0 0.7 copy.20
  122.7 1.3 %copy.21 = bf16[256,4096]{1,0:T(8,128)(2,1)} copy(bf16[256,4096]{1,0:T(8,128)(2,1)S(1)} %get-tuple-element.34) | data formatting | bytes 4194304
  (7 shorter events, 0.1 us)
Async XLA Ops:
  0.6 4.0 %copy-start.2 = (bf16[256,512]{1,0:T(8,128)(2,1)S(1)}, bf16[256,512]{1,0:T(8,128)(2,1)}, u32[]{:S(2)}) copy-start(bf16[256,512]{1,0:T(8,128)(2,1)} %tok_ref.1) | copy-start | bytes 786436
  2.5 34.4 %copy-start.4 = (s32[256]{0:T(256)S(1)}, s32[256]{0:T(256)}, u32[]{:S(2)}) copy-start(s32[256]{0:T(256)} %param.10) | copy-start | bytes 3076
  2.5 34.4 %copy-start.3 = (bf16[256,512]{1,0:T(8,128)(2,1)S(1)}, bf16[256,512]{1,0:T(8,128)(2,1)}, u32[]{:S(2)}) copy-start(bf16[256,512]{1,0:T(8,128)(2,1)} %param.11) | copy-start | bytes 786436
  34.8 1.3 %copy-start = (bf16[8,256,512]{2,1,0:T(8,128)(2,1)}, bf16[8,256,512]{2,1,0:T(8,128)(2,1)S(1)}, u32[]{:S(2)}) copy-start(bf16[8,256,512]{2,1,0:T(8,128)(2,1)S(1)} %get-tuple-element.11.tok_ref) | copy-start | bytes 6291460
  56.8 1.3 %copy-start.1 = (bf16[8,256,512]{2,1,0:T(8,128)(2,1)}, bf16[8,256,512]{2,1,0:T(8,128)(2,1)S(1)}, u32[]{:S(2)}) copy-start(bf16[8,256,512]{2,1,0:T(8,128)(2,1)S(1)} %get-tuple-element.15.gi_ref) | copy-start | bytes 6291460

commit v5 on v4

--- a/solution.py
+++ b/solution.py
@@ -370,45 +370,73 @@
     def peer(i):
         return lax.rem(me + i, n_mp)
 
-    def copies(i, slot):
+    def twin(i):
+        return i + 1 - 2 * lax.rem(i, 2)
+
+    def pay(i, slot):
         d = peer(i)
-        return (
-            pltpu.make_async_remote_copy(
-                src_ref=pay_ref.at[d], dst_ref=pay_out.at[slot],
-                send_sem=p_send.at[d], recv_sem=p_recv.at[slot],
-                device_id={"mp": d}, device_id_type=MESH),
-            pltpu.make_async_remote_copy(
-                src_ref=tok_ref, dst_ref=tok_out.at[slot],
-                send_sem=t_send.at[d], recv_sem=t_recv.at[slot],
-                device_id={"mp": d}, device_id_type=MESH),
-        )
+        return pltpu.make_async_remote_copy(
+            src_ref=pay_ref.at[d], dst_ref=pay_out.at[slot],
+            send_sem=p_send.at[d], recv_sem=p_recv.at[slot],
+            device_id={"mp": d}, device_id_type=MESH)
+
+    def far(q, slot):
+        d = peer(2 * q)
+        return pltpu.make_async_remote_copy(
+            src_ref=tok_ref, dst_ref=tok_out.at[slot],
+            send_sem=t_send.at[d], recv_sem=t_recv.at[slot],
+            device_id={"mp": d}, device_id_type=MESH)
+
+    def near(src, sent, slot):
+        return pltpu.make_async_remote_copy(
+            src_ref=src, dst_ref=tok_out.at[slot],
+            send_sem=t_send.at[twin(sent)], recv_sem=t_recv.at[slot],
+            device_id={"mp": twin(me)}, device_id_type=MESH)
 
     def greet(i, _):
         pl.semaphore_signal(barrier, inc=1, device_id={"mp": peer(i)}, device_id_type=MESH)
         return 0
 
-    def start(i, _):
-        for copy in copies(i, me):
-            copy.start()
-        return 0
-
-    def arrive(i, _):
-        for copy in copies(i, peer(i)):
-            copy.wait_recv()
-        return 0
-
-    def leave(i, _):
-        for copy in copies(i, me):
-            copy.wait_send()
+    def start_pay(i, _):
+        pay(i, me).start()
+        return 0
+
+    def start_far(q, _):
+        far(q, me).start()
+        return 0
+
+    def hand_on(q, _):
+        d = peer(2 * q)
+        far(q, d).wait_recv()
+        near(tok_out.at[d], d, d).start()
+        return 0
+
+    def arrive(q, _):
+        near(tok_ref, me, twin(peer(2 * q))).wait_recv()
+        return 0
+
+    def finish(i, _):
+        pay(i, peer(i)).wait_recv()
+        pay(i, me).wait_send()
+        return 0
+
+    def leave(q, _):
+        far(q, me).wait_send()
+        near(tok_out.at[peer(2 * q)], peer(2 * q), peer(2 * q)).wait_send()
         return 0
 
     lax.fori_loop(1, n_mp, greet, 0)
     pl.semaphore_wait(barrier, n_mp - 1)
-    lax.fori_loop(1, n_mp, start, 0)
+    lax.fori_loop(1, n_mp, start_pay, 0)
+    lax.fori_loop(1, n_mp // 2, start_far, 0)
+    near(tok_ref, me, me).start()
     tok_out[me] = tok_ref[...]
     pay_out[me] = pay_ref[me]
-    lax.fori_loop(1, n_mp, arrive, 0)
-    lax.fori_loop(1, n_mp, leave, 0)
+    lax.fori_loop(1, n_mp // 2, hand_on, 0)
+    lax.fori_loop(0, n_mp // 2, arrive, 0)
+    lax.fori_loop(1, n_mp, finish, 0)
+    lax.fori_loop(1, n_mp // 2, leave, 0)
+    near(tok_ref, me, me).wait_send()
 
 
 def gather_call(tokens, payload):

time: 124 us -> 115 us (0.927)
  Pallas kernels: 113 us -> 105 us
    pallas_call x1, Pallas kernels: 30.1 us -> 21.9 us  [gather_call(): pl.pallas_call(gather_kernel, out_shape=(jax.ShapeDtypeStruct((n_mp,) + t...]
where the time goes in v5:
time: 115 us
  Pallas kernels  105 us (91%)
  local copies, waits for them, and re-layouts  5.38 us (5%)
  other arithmetic  2.34 us (2%)
  matrix products  2.02 us (2%)
    pallas_call x1, Pallas kernels, reduce_call(): pl.pallas_call(functools.partial(reduce_kernel, scale), out_shape=(jax.Sh...  63 us
    pallas_call x1, Pallas kernels, gather_call(): pl.pallas_call(gather_kernel, out_shape=(jax.ShapeDtypeStruct((n_mp,) + t...  21.9 us
    pallas_call x1, Pallas kernels, dense_call(): pl.pallas_call(dense_kernel, out_shape=(jax.ShapeDtypeStruct((tok_count,...  19.8 us
    unnamed x12, local copies, waits for them, and re-layouts  4.67 us

profile of v5, /device:TPU:0, one launch (start us, length us, event | category | flops | bytes accessed | tf_op | source)
XLA Modules:
  0.0 115.2 jit_solution(1828689293824286139)
XLA Ops:
  0.6 0.0 copy-start.2
  0.6 0.8 fusion.19
  1.4 0.2 convert_reduce_fusion
  1.6 0.8 select_reduce_fusion.1
  2.4 0.1 copy.16
  2.5 0.0 copy-start.4
  2.5 0.0 copy-start.3
  2.5 2.0 %convolution_convert_fusion = bf16[24,4096]{1,0:T(8,128)(2,1)S(1)} fusion(bf16[256,4096]{1,0:T(8,128)(2,1)} %w_ref.1, s32[256]{0:T(256)S(1)} %add_select_fusion.2), kind=kOutput, calls=%fused_computation | convolution fusion | flops 50436096 | bytes 2294784 | tf_op jit(solution)/shard_map/dot_general | solution.py:490
  4.6 0.1 reshape.135.pay_ref
  4.7 0.0 copy-done.2
  4.7 21.9 %gather.1 = (bf16[8,256,512]{2,1,0:T(8,128)(2,1)S(1)}, bf16[8,3,4224]{2,1,0:T(4,128)(2,1)S(1)}) custom-call(bf16[256,512]{1,0:T(8,128)(2,1)S(1)} %copy-done.2, bf16[8,3,4224]{2,1,0:T(4,128)(2,1)S(1)} %reshape.135.pay_ref), custom_call_target="tpu_custom_call" | custom-call | tf_op jit(solution)/shard_map/gather/pallas_call | solution.py:446
  26.6 0.0 copy-start
  26.6 1.3 %copy-done = bf16[8,256,512]{2,1,0:T(8,128)(2,1)} copy-done((bf16[8,256,512]{2,1,0:T(8,128)(2,1)}, bf16[8,256,512]{2,1,0:T(8,128)(2,1)S(1)}, u32[]{:S(2)}) %copy-start) | copy-done | bytes 2097176
  27.9 0.2 reshape.136
  28.0 0.2 convert_reduce_fusion.1
  28.2 0.2 fusion.17
  28.5 0.1 copy.17.ccol_ref
  28.6 0.0 copy-done.4
  28.6 0.0 copy-done.3
  28.6 0.1 multiply_convert_fusion.up_ref
  28.8 19.8 %dense.1 = (bf16[256,512]{1,0:T(8,128)(2,1)}, bf16[8,256,512]{2,1,0:T(8,128)(2,1)S(1)}, bf16[256,4096]{1,0:T(8,128)(2,1)S(1)}, bf16[24,4096]{1,0:T(8,128)(2,1)S(1)}) custom-call(bf16[8,256,512]{2,1,0:T(8,128)(2,1)} %copy-done, bf16[256,512]{1,0:T(8,128)(2,1)S(1)} %multiply_convert_fusion.up_ref, bf16[256,4096]{1,0:T(8,128)(2,1)} %w_ref.1, ...), custom_call_target="tpu_custom_call" | custom-call | tf_op jit(solution)/shard_map/dense/pallas_call | solution.py:105
  48.6 0.0 copy-start.1
  48.6 1.3 %copy-done.1 = bf16[8,256,512]{2,1,0:T(8,128)(2,1)} copy-done((bf16[8,256,512]{2,1,0:T(8,128)(2,1)}, bf16[8,256,512]{2,1,0:T(8,128)(2,1)S(1)}, u32[]{:S(2)}) %copy-start.1) | copy-done | bytes 2097176
  49.9 0.1 reshape.137.gin_ref
  50.0 0.1 slice.22
  50.1 0.1 fusion.3.hot_ref
  50.2 63.0 %reduce.7 = (bf16[256,4096]{1,0:T(8,128)(2,1)S(1)}, bf16[256,512]{1,0:T(8,128)(2,1)S(1)}) custom-call(bf16[256,4096]{1,0:T(8,128)(2,1)S(1)} %get-tuple-element.14.gw_ref, bf16[8,256,512]{2,1,0:T(8,128)(2,1)} %copy-done.1, bf16[8,3,4096]{2,1,0:T(4,128)(2,1)S(1)} %reshape.137.gin_ref, bf16[32,24]{1,0:T(8,128)(2,1)S(1)} %fusion.3.hot_ref), custom_call_target="tpu_custom_call" | custom-call | tf_op jit(solution)/shard_map/reduce/pallas_call | solution.py:340
  113.2 0.7 copy.20
  113.9 1.3 %copy.21 = bf16[256,4096]{1,0:T(8,128)(2,1)} copy(bf16[256,4096]{1,0:T(8,128)(2,1)S(1)} %get-tuple-element.34) | data formatting | bytes 4194304
  (7 shorter events, 0.1 us)
Async XLA Ops:
  0.6 4.0 %copy-start.2 = (bf16[256,512]{1,0:T(8,128)(2,1)S(1)}, bf16[256,512]{1,0:T(8,128)(2,1)}, u32[]{:S(2)}) copy-start(bf16[256,512]{1,0:T(8,128)(2,1)} %tok_ref.1) | copy-start | bytes 786436
  2.5 26.1 %copy-start.4 = (s32[256]{0:T(256)S(1)}, s32[256]{0:T(256)}, u32[]{:S(2)}) copy-start(s32[256]{0:T(256)} %param.10) | copy-start | bytes 3076
  2.5 26.1 %copy-start.3 = (bf16[256,512]{1,0:T(8,128)(2,1)S(1)}, bf16[256,512]{1,0:T(8,128)(2,1)}, u32[]{:S(2)}) copy-start(bf16[256,512]{1,0:T(8,128)(2,1)} %param.11) | copy-start | bytes 786436
  26.6 1.3 %copy-start = (bf16[8,256,512]{2,1,0:T(8,128)(2,1)}, bf16[8,256,512]{2,1,0:T(8,128)(2,1)S(1)}, u32[]{:S(2)}) copy-start(bf16[8,256,512]{2,1,0:T(8,128)(2,1)S(1)} %get-tuple-element.11.tok_ref) | copy-start | bytes 6291460
  48.6 1.3 %copy-start.1 = (bf16[8,256,512]{2,1,0:T(8,128)(2,1)}, bf16[8,256,512]{2,1,0:T(8,128)(2,1)S(1)}, u32[]{:S(2)}) copy-start(bf16[8,256,512]{2,1,0:T(8,128)(2,1)S(1)} %get-tuple-element.15.gi_ref) | copy-start | bytes 6291460
